TPU v7x, 32 devices: a whole 2x2x4 slice. The times are simulated.
32 devices in a mesh: outer: 8 (over z, y), inner: 4 (over x, core).
Axes of the slice: x: 2, y: 2, z: 4, core: 2. Of those that a mesh axis runs over, the one named last changes fastest.
Arguments:
- hidden: bfloat16 [4096, 1024], P(('outer', 'inner')), may hold values from -6 to 6
- x_act: bfloat16 [4096, 2048], P(('outer', 'inner')), may hold values from -6 to 6
- dt_step: float32 [4096, 32], P(('outer', 'inner')), may hold values from 0.00421875 to 0.44, as said below
- log_decay: float32 [4096, 32], P(('outer', 'inner')), may hold values from -0.81 to -7.080078e-06, as said below
- w_bc: bfloat16 [1024, 128], P(('outer', 'inner')), may hold values from -0.1875 to 0.1875
- grad_y: bfloat16 [4096, 2048], P(('outer', 'inner')), may hold values from -0.19921875 to 0.19921875
Outputs:
- grad_x: float32 [4096, 2048], P(('outer', 'inner'))
- grad_hidden: float32 [4096, 1024], P(('outer', 'inner'))
- grad_proj: float32 [1024, 128], P(('outer', 'inner'))
Inputs may be any that keep to these rules, and one draw needn't show every extreme that they name: `dt_step`: Positive; constant in scale within each head apart from a factor within e**-0.5 to e**0.5. `log_decay`: Negative.
All inputs are finite; a program needn't handle non-finite values.
Results may differ from a plain program's by a relative error of at most 0.0029.
Values may be sent and summed in bfloat16 or wider, within the bound.
No kernel may reach another device: no remote copies, remote signals or barrier semaphores. Data moves between devices by JAX's collectives and lax.ppermute only.
A program may use at most 64 MiB of HBM per device.

v0:
```python
import math

import jax
import jax.numpy as jnp
from jax import lax
from jax.sharding import PartitionSpec as P

BLOCK = 128


HIGH = lax.Precision.HIGHEST


def carried_in(array, axis, combine, identity, reverse):
    count, mine = (lax.axis_size(axis), lax.axis_index(axis))
    everything = jax.tree.map(lambda part: lax.all_gather(part, axis), array)
    start = jax.tree.map(
        lambda part, zero: jnp.broadcast_to(jnp.asarray(zero, part.dtype), part.shape),
        array,
        identity,
    )

    def step(k, before):
        at = count - 1 - k if reverse else k
        reached = at > mine if reverse else at < mine
        new = combine(before, jax.tree.map(lambda part: part[at], everything))
        return jax.tree.map(lambda a, b: jnp.where(reached, a, b), new, before)

    return lax.fori_loop(0, count, step, start)


def block_step(carried, pieces):
    inputs, decays, b_rows, c_rows = pieces
    length = inputs.shape[0]
    running = jnp.cumsum(decays, axis=0)
    row_ids = lax.broadcasted_iota(jnp.int32, (length, length), 0)
    col_ids = lax.broadcasted_iota(jnp.int32, (length, length), 1)
    causal = row_ids >= col_ids
    spread = running.T[:, :, None] - running.T[:, None, :]
    segment = jnp.where(causal[None], jnp.exp(jnp.where(causal[None], spread, 0.0)), 0.0)
    scores = jnp.einsum("in,jn->ij", c_rows, b_rows, precision=HIGH)
    outputs = jnp.einsum("hij,jhp->ihp", segment * scores[None], inputs, precision=HIGH)
    outputs = outputs + jnp.exp(running)[:, :, None] * jnp.einsum(
        "in,hpn->ihp", c_rows, carried, precision=HIGH
    )
    final_sum = running[-1]
    weights = jnp.exp(final_sum[None, :] - running)
    updated = jnp.exp(final_sum)[:, None, None] * carried + jnp.einsum(
        "jhp,jn->hpn", inputs * weights[:, :, None], b_rows, precision=HIGH
    )
    return (updated, outputs)


def scan_block(inputs, decays, b_rows, c_rows, carried, length):
    count = inputs.shape[0] // length
    pieces = (
        inputs.reshape((count, length) + inputs.shape[1:]),
        decays.reshape((count, length, decays.shape[1])),
        b_rows.reshape((count, length, b_rows.shape[1])),
        c_rows.reshape((count, length, c_rows.shape[1])),
    )
    final_state, outputs = lax.scan(block_step, carried, pieces)
    return (outputs.reshape(inputs.shape), final_state)


def slice_combine(earlier, later):
    return (earlier[0] + later[0], jnp.exp(later[0])[:, None] * earlier[1] + later[1])


def slice_step(carry, item):
    return (slice_combine(carry, item), carry)


def per_device(hidden, x_act, dt_step, log_decay, w_bc, grad_y):
    weights_full = lax.all_gather(w_bc, ("outer", "inner"), axis=0, tiled=True)
    state_width = weights_full.shape[1] // 2
    row_count = hidden.shape[0]
    head_count = dt_step.shape[1]
    head_size = x_act.shape[1] // head_count
    projected = jnp.dot(hidden, weights_full, preferred_element_type=jnp.float32)
    b_rows = projected[:, :state_width]
    c_rows = projected[:, state_width:]
    inputs = dt_step[:, :, None] * x_act.astype(jnp.float32).reshape(
        row_count, head_count, head_size
    )
    cotangent = grad_y.astype(jnp.float32).reshape(row_count, head_count, head_size)
    running = jnp.cumsum(log_decay, axis=0)
    totals = running[-1]
    own_state = jnp.einsum(
        "jhp,jn->hpn",
        inputs * jnp.exp(totals[None, :] - running)[:, :, None],
        b_rows,
        precision=HIGH,
    )
    own_adjoint = jnp.einsum(
        "ihp,in->hpn", cotangent * jnp.exp(running)[:, :, None], c_rows, precision=HIGH
    )
    inner_count = lax.axis_size("inner")
    flat_width = head_size * state_width
    paired = jnp.stack(
        [own_state.reshape(head_count, flat_width), own_adjoint.reshape(head_count, flat_width)]
    )[None]
    totals_wide = jnp.broadcast_to(totals[None, None, :, None], (1, 1, head_count, inner_count))
    slices, all_totals = (
        lax.all_to_all(paired, "inner", split_axis=3, concat_axis=0, tiled=True),
        lax.all_to_all(totals_wide, "inner", split_axis=3, concat_axis=0, tiled=True),
    )
    all_totals = all_totals[:, 0, :, 0]
    zero_slice = (jnp.zeros((head_count,), jnp.float32), jnp.zeros_like(slices[0, 0]))
    forward_total, forward_prior = lax.scan(slice_step, zero_slice, (all_totals, slices[:, 0]))
    backward_total, backward_after = lax.scan(
        slice_step, zero_slice, (all_totals, slices[:, 1]), reverse=True
    )
    coarse_forward = carried_in(forward_total, "outer", slice_combine, zero_slice, False)
    coarse_backward = carried_in(backward_total, "outer", slice_combine, zero_slice, True)
    state_part = jnp.exp(forward_prior[0])[:, :, None] * coarse_forward[1][None] + forward_prior[1]
    adjoint_part = (
        jnp.exp(backward_after[0])[:, :, None] * coarse_backward[1][None] + backward_after[1]
    )
    returned = lax.all_to_all(
        jnp.stack([state_part, adjoint_part], 1), "inner", split_axis=0, concat_axis=3, tiled=True
    )
    state_in = returned[0, 0].reshape(head_count, head_size, state_width)
    adjoint_out = returned[0, 1].reshape(head_count, head_size, state_width)

    def forward(inputs, b_rows, c_rows):
        return scan_block(inputs, log_decay, b_rows, c_rows, state_in, BLOCK)

    outputs, pullback = jax.vjp(forward, inputs, b_rows, c_rows)
    d_in, d_b, d_c = pullback((cotangent, adjoint_out))
    grad_x = (dt_step[:, :, None] * d_in).reshape(row_count, head_count * head_size)
    d_proj = jnp.concatenate([d_b, d_c], axis=1)
    d_low = d_proj.astype(jnp.bfloat16)
    grad_hidden = lax.dot_general(
        d_low, weights_full, (((1,), (1,)), ((), ())), preferred_element_type=jnp.float32
    )
    scale = 1.0 / math.sqrt(row_count * lax.axis_size("outer") * lax.axis_size("inner"))
    grad_proj = lax.psum_scatter(
        lax.dot_general(hidden, d_low, (((0,), (0,)), ((), ())), preferred_element_type=jnp.float32)
        * scale,
        ("outer", "inner"),
        scatter_dimension=0,
        tiled=True,
    )
    return (grad_x, grad_hidden, grad_proj)


def solution(mesh):
    in_specs = (
        P(("outer", "inner"), None),
        P(("outer", "inner"), None),
        P(("outer", "inner"), None),
        P(("outer", "inner"), None),
        P(("outer", "inner"), None),
        P(("outer", "inner"), None),
    )
    out_specs = (
        P(("outer", "inner"), None),
        P(("outer", "inner"), None),
        P(("outer", "inner"), None),
    )
    return jax.shard_map(
        per_device, mesh=mesh, in_specs=in_specs, out_specs=out_specs, check_vma=False
    )
```

profile of v0, /device:TPU:0, one launch (start us, length us, event | category | flops | bytes accessed | tf_op | source)
XLA Modules:
  0.0 382.8 jit_solution(757989280330233703)
XLA Ops:
  7.2 0.9 copy.63
  8.3 44.2 %all_gather.27 = bf16[1024,128]{1,0:T(8,128)(2,1)S(1)} all-gather(bf16[32,128]{1,0:T(8,128)(2,1)} %param.18), channel_id=1, replica_groups=mesh['outer'=8,'inner'=4] {'outer','inner'}, dimensions={0}, use_global_device_ids=true | all-gather | bytes 270336 | tf_op jit(solution)/shard_map/all_gather | solution.py:75
  52.5 1.4 copy.64
  54.3 1.0 fusion.29
  56.3 1.0 fusion.27
  57.7 4.4 %copy.68 = f32[2,32,4096]{1,0,2:T(2,128)} copy(f32[2,32,4096]{2,1,0:T(8,128)S(1)} %pad_maximum_fusion) | data formatting | bytes 2097152 | tf_op jit(solution)/shard_map/stack | solution.py:100
  62.1 4.7 %bitcast_bitcast_fusion = f32[4096,1,2,32]{3,2,1,0:T(2,128)} fusion(f32[2,32,4096]{1,0,2:T(2,128)} %copy.68), kind=kLoop, calls=%fused_computation.87 | loop fusion | bytes 2097152
  66.8 6.5 %reshape.273 = f32[4,1,65536]{2,1,0:T(1,128)} reshape(f32[4096,1,2,32]{3,2,1,0:T(2,128)} %bitcast_bitcast_fusion) | data formatting | bytes 2097152
  73.3 4.4 %all-to-all-start.1 = ((f32[4,1,65536]{2,1,0:T(1,128)}), f32[4,1,65536]{2,1,0:T(1,128)}, u32[]{:S(2)}, u32[]{:S(2)}) async-start(f32[4,1,65536]{2,1,0:T(1,128)} %reshape.273), calls=%async_computation.1 | async-start | bytes 2097152 | tf_op jit(solution)/shard_map/all_to_all | solution.py:105
  78.9 13.3 %all-to-all-done.1 = f32[4,1,65536]{2,1,0:T(1,128)} async-done(((f32[4,1,65536]{2,1,0:T(1,128)}), f32[4,1,65536]{2,1,0:T(1,128)}, u32[]{:S(2)}, u32[]{:S(2)}) %all-to-all-start.1) | async-done | bytes 1048608 | tf_op jit(solution)/shard_map/all_to_all | solution.py:105
  92.8 3.8 all-to-all-start
  97.4 4.6 %reduce = f32[4,65536]{1,0:T(4,128)S(1)} reduce(f32[4,1,65536]{2,1,0:T(1,128)} %all-to-all-done.1, f32[]{:T(128)} %broadcast.232), dimensions={1}, to_apply=%all_to_all.40.reduce_sub_computation | reduce | bytes 2097156 | tf_op jit(solution)/shard_map/all_to_all | solution.py:105
  102.0 5.6 %reshape.274 = f32[4096,1,2,32]{3,2,1,0:T(2,128)} reshape(f32[4,65536]{1,0:T(4,128)S(1)} %reduce) | data formatting | bytes 2097152
  107.6 5.3 %copy.86 = f32[1,2,32,4,1024]{4,3,2,1,0:T(4,128)S(1)} copy(f32[1,2,32,4,1024]{2,1,4,3,0:T(2,128)} %bitcast.151) | data formatting | bytes 2097152 | tf_op jit(solution)/shard_map/all_to_all | solution.py:105
  112.9 0.9 slice_bitcast_fusion.1
  113.8 10.5 %while.88 = (s32[]{:T(128)}, f32[32]{0:T(128)}, f32[32,1024]{1,0:T(8,128)S(1)}, f32[4,32]{1,0:T(4,128)S(1)}, f32[4,32,1024]{2,1,0:T(8,128)S(1)}, /*index=5*/f32[...) while((s32[]{:T(128)}, f32[32]{0:T(128)}, f32[32,1024]{1,0:T(8,128)S(1)}, ...), condition=%wide.region_2.3_spmd.clone, body=%wide.region_1.2_spmd.clone.sunk | while | flops 131139 | bytes 918649 | solution.py:110
  113.9 1.3 fusion.77
  115.2 1.2 constant_dynamic-slice_fusion.6
  116.5 1.3 fusion.77
  117.8 1.2 constant_dynamic-slice_fusion.6
  119.1 1.3 fusion.77
  120.4 1.2 constant_dynamic-slice_fusion.6
  121.7 1.3 fusion.77
  123.0 1.2 constant_dynamic-slice_fusion.6
  125.1 0.9 dynamic-update-slice
  126.1 6.0 %while.90 = (s32[]{:T(128)}, f32[32]{0:T(128)}, f32[32,1024]{1,0:T(8,128)S(1)}, f32[4,32]{1,0:T(4,128)S(1)}, f32[4,32,1024]{2,1,0:T(8,128)S(1)}, /*index=5*/f32[...) while((s32[]{:T(128)}, f32[32]{0:T(128)}, ...), condition=%wide.region_6.7_spmd.clone, body=%wide.region_5.6_spmd.clone.sunk | while | flops 131140 | bytes 918669 | solution.py:111
  126.1 1.2 fusion.80
  127.6 1.2 fusion.80
  129.1 1.2 fusion.80
  130.6 1.2 fusion.80
  132.9 17.3 %all-reduce.2 = (f32[256]{0:T(256)S(1)}, f32[256]{0:T(256)S(1)}) all-reduce(f32[256]{0:T(256)S(1)} %dynamic-update-slice.1, f32[256]{0:T(256)S(1)} %dynamic-update-slice), channel_id=4, replica_groups=mesh['outer'=8,'inner'=4] {'outer'}, use_global_device_ids=true, to_apply=%add.1 | all-reduce | flops 512 | bytes 4096
  150.4 13.0 %all-gather.7.cloned.1.call-done = f32[256,1024]{1,0:T(8,128)} async-done(((f32[32,1024]{1,0:T(8,128)}), f32[256,1024]{1,0:T(8,128)}) %all-gather.7.cloned.1.call-update) | async-done | bytes 1048592 | tf_op jit(solution)/shard_map/all_gather | solution.py:16
  163.3 8.2 %while.89 = (s32[]{:T(128)}, f32[32,1024]{1,0:T(8,128)S(1)}, s32[]{:T(128)}, f32[8,32]{1,0:T(8,128)S(1)}, f32[8,32,1024]{2,1,0:T(8,128)}, /*index=5*/s32[]{:T(128)}, s32[]{:T(128)}) while((s32[]{:T(128)}, f32[32,1024]{1,0:T(8,128)S(1)}, s32[]{:T(128)}, f32[8,32]{1,0:T(8,128)S(1)}, f32[8,32,1024]{2,1,0:T(8,128)}, ...), condition=%wide.region_4.5_spmd.clone, body=%wide.region_3.4_spmd.clone.sunk | while | flops 131076 | bytes 393705 | solution.py:29
  163.4 1.0 fusion.79
  164.4 1.0 fusion.79
  165.4 1.0 fusion.79
  166.5 1.0 fusion.79
  167.5 1.0 fusion.79
  168.5 1.0 fusion.79
  169.6 1.0 fusion.79
  170.6 1.0 fusion.79
  171.6 33.3 %all-gather.9.cloned.1.call-done = f32[256,1024]{1,0:T(8,128)} async-done(((f32[32,1024]{1,0:T(8,128)}), f32[256,1024]{1,0:T(8,128)}) %all-gather.9.cloned.1.call-update) | async-done | bytes 1048592 | tf_op jit(solution)/shard_map/all_gather | solution.py:16
  204.9 8.3 %while.91 = (s32[]{:T(128)}, f32[32,1024]{1,0:T(8,128)S(1)}, s32[]{:T(128)}, f32[8,32]{1,0:T(8,128)S(1)}, f32[8,32,1024]{2,1,0:T(8,128)}, /*index=5*/s32[]{:T(128)}, s32[]{:T(128)}, s32[]{:T(128)}, s32[]{:T(128)}) while((s32[]{:T(128)}, f32[32,1024]{1,0:T(8,128)S(1)}, s32[]{:T(128)}, f32[8,32]{1,0:T(8,128)S(1)}, ...), condition=%wide.region_8.9_spmd.clone, body=%wide.region_7.8_spmd.clone.sunk | while | flops 131080 | bytes 393767 | solution.py:29
  204.9 1.0 fusion.82
  205.9 1.0 fusion.82
  207.0 1.0 fusion.82
  208.0 1.0 fusion.82
  209.1 1.0 fusion.82
  210.1 1.0 fusion.82
  211.2 1.0 fusion.82
  212.2 1.0 fusion.82
  213.4 1.1 pad_maximum_fusion.1
  214.5 3.5 all-to-all-start.2
  218.3 1.0 bitcast_multiply_fusion.3
  219.7 3.5 fusion.15
  223.2 2.4 fusion.12
  225.7 6.7 %all-to-all-done.2 = f32[4,2,32,1024]{3,2,1,0:T(8,128)S(1)} async-done(((f32[4,2,32,1024]{3,2,1,0:T(8,128)}), f32[4,2,32,1024]{3,2,1,0:T(8,128)S(1)}, u32[]{:S(2)}, u32[]{:S(2)}) %all-to-all-start.2) | async-done | bytes 1048608 | tf_op jit(solution)/shard_map/all_to_all | solution.py:120
  233.0 2.2 fusion.18
  235.4 1.9 convolution_bitcast_fusion.1
  238.0 3.1 convolution_bitcast_fusion
  241.5 1.0 copy.87
  242.6 1.3 copy.80
  243.9 1.0 fusion.49
  244.9 131.4 %reduce-scatter.4.cloned.1.call-done = f32[32,128]{1,0:T(8,128)} async-done(((f32[1024,128]{1,0:T(8,128)}), f32[32,128]{1,0:T(8,128)}) %reduce-scatter.4.cloned.1.call-update) | async-done | bytes 16400
  (125 shorter events, 10.1 us)
Async XLA Ops:
  7.2 46.8 %copy-start = (bf16[128,1024]{1,0:T(8,128)(2,1)S(1)}, bf16[128,1024]{1,0:T(8,128)(2,1)}, u32[]{:S(2)}) copy-start(bf16[128,1024]{1,0:T(8,128)(2,1)} %param.14) | copy-start | bytes 786436
  7.2 47.1 %copy-start.8 = (f32[128,32]{0,1:T(8,128)S(1)}, f32[128,32]{0,1:T(8,128)}, u32[]{:S(2)}) copy-start(f32[128,32]{0,1:T(8,128)} %param.16) | copy-start | bytes 49156
  8.2 47.4 %copy-start.13 = (f32[32]{0:T(128)}, f32[32]{0:T(128)S(1)}, u32[]{:S(2)}) copy-start(f32[32]{0:T(128)S(1)} %slice_bitcast_fusion.2) | copy-start | bytes 388
  52.5 1.7 copy-start.3
  53.9 1.7 copy-start.5
  55.7 0.6 copy-start.6
  73.3 4.5 %copy-start.15 = (u32[32]{0:T(128)S(1)}, u32[32]{0:T(128)}, u32[]{:S(2)}) copy-start(u32[32]{0:T(128)} %constant.201) | copy-start | bytes 388
  73.3 18.9 %copy-start.14 = (f32[32]{0:T(128)S(1)}, f32[32]{0:T(128)}, u32[]{:S(2)}) copy-start(f32[32]{0:T(128)} %copy-done.13) | copy-start | bytes 388
  73.3 18.9 %all-to-all-start.1 = ((f32[4,1,65536]{2,1,0:T(1,128)}), f32[4,1,65536]{2,1,0:T(1,128)}, u32[]{:S(2)}, u32[]{:S(2)}) async-start(f32[4,1,65536]{2,1,0:T(1,128)} %reshape.273), calls=%async_computation.1 | async-start | bytes 2097152 | tf_op jit(solution)/shard_map/all_to_all | solution.py:105
  92.8 21.0 %all-to-all-start = ((f32[1,1,32,4]{2,1,0,3:T(1,128)}), f32[1,1,32,4]{2,1,0,3:T(1,128)}, u32[]{:S(2)}, u32[]{:S(2)}) async-start(f32[1,1,32,4]{2,1,0,3:T(1,128)} %broadcast_in_dim.120), calls=%async_computation | async-start | bytes 4096 | tf_op jit(solution)/shard_map/all_to_all | solution.py:106
  96.6 66.7 %all-gather.7.cloned.1.call-start = ((), (), s32[]{:S(2)}) async-start(), calls=%async_computation.4 | async-start | bytes 1179648 | tf_op jit(solution)/shard_map/all_gather | solution.py:16
  124.4 0.7 copy-start.2
  124.4 1.6 copy-start.11
  125.0 79.9 %all-gather.9.cloned.1.call-start = ((), (), s32[]{:S(2)}) async-start(), calls=%async_computation.5 | async-start | bytes 1179648 | tf_op jit(solution)/shard_map/all_gather | solution.py:16
  126.0 24.3 %copy-start.12 = (f32[4,32]{1,0:T(4,128)S(1)}, f32[4,32]{1,0:T(4,128)}, u32[]{:S(2)}) copy-start(f32[4,32]{1,0:T(4,128)} %copy-done.11) | copy-start | bytes 1540
  132.1 18.3 %copy-start.1 = (f32[32,1024]{1,0:T(8,128)}, f32[32,1024]{1,0:T(8,128)S(1)}, u32[]{:S(2)}) copy-start(f32[32,1024]{1,0:T(8,128)S(1)} %get-tuple-element.577) | copy-start | bytes 393220
  213.4 4.9 %copy-start.7 = (f32[128,32]{0,1:T(8,128)S(1)}, f32[128,32]{0,1:T(8,128)}, u32[]{:S(2)}) copy-start(f32[128,32]{0,1:T(8,128)} %copy-done.6) | copy-start | bytes 49156
  214.5 17.9 %all-to-all-start.2 = ((f32[4,2,32,1024]{3,2,1,0:T(8,128)}), f32[4,2,32,1024]{3,2,1,0:T(8,128)S(1)}, u32[]{:S(2)}, u32[]{:S(2)}) async-start(f32[4,2,32,1024]{3,2,1,0:T(8,128)} %pad_maximum_fusion.1), calls=%async_computation.2 | async-start | bytes 2097152 | tf_op jit(solution)/shard_map/all_to_all | solution.py:120
  218.0 158.3 %reduce-scatter.4.cloned.1.call-start = ((), (), s32[]{:S(2)}) async-start(), calls=%async_computation.6 | async-start | bytes 540672
  219.7 3.5 copy-start.9
  233.0 2.3 copy-start.10
  241.3 2.6 copy-start.4
Sparse Core Ops, SparseCore 0:
  125.2 38.1 all-gather.6
  166.0 38.8 all-gather.8
  242.7 133.5 reduce-scatter.3
where the time goes:
time: 384 us; the launch traced here: 383 us
  waiting for transfers between devices  198 us (52%)
  blocking collectives  61.5 us (16%)
  local copies, waits for them, and re-layouts  44.6 us (12%)
  other arithmetic  34 us (9%)
  matrix products  17.4 us (5%)
  between operations  14.8 us (4%)
  starting transfers between devices  12.3 us (3%)
    unnamed x4, waiting for transfers between devices  131 us
    all_gather x2, waiting for transfers between devices, carried_in(): everything = jax.tree.map(lambda part: lax.all_gather(part, axis), array)  46.3 us
    all_gather x1, blocking collectives, per_device(): weights_full = lax.all_gather(w_bc, ('outer', 'inner'), axis=0, tiled=True)  44.2 us
    unnamed x45, local copies, waits for them, and re-layouts  25 us
    unnamed x1, blocking collectives  17.3 us
    select_n x16, other arithmetic, step(): return jax.tree.map(lambda a, b: jnp.where(reached, a, b), new, before)  15.9 us
    all_to_all x1, waiting for transfers between devices, per_device(): lax.all_to_all(paired, 'inner', split_axis=3, concat_axis=0, tiled=True)  13.3 us
    exp x8, other arithmetic, slice_combine(): jnp.exp(later[0])[:, None] * earlier[1] + later[1]  9.94 us
  transfers between devices with their start and end apart: 6, of which 5 were waited for; matrix products, arithmetic and copies ran while one was open for 11% of the time, Pallas kernels for 0%

commit v1 on v0

v1 whole, which is shorter than its diff:
```python
import functools
import math

import jax
import jax.numpy as jnp
from jax import lax
from jax.experimental import pallas as pl
from jax.experimental.pallas import tpu as pltpu
from jax.sharding import PartitionSpec as P

AXES = ("outer", "inner")
HIGH = lax.Precision.HIGHEST
F32 = jnp.float32
BF16 = jnp.bfloat16
NEG = -1e30
VMEM = pl.BlockSpec(memory_space=pltpu.MemorySpace.VMEM)
SMEM = pl.BlockSpec(memory_space=pltpu.MemorySpace.SMEM)
HBM = pl.BlockSpec(memory_space=pltpu.MemorySpace.HBM)


def call(kernel, name, out_shape, in_specs, scratch=(), out_specs=None):
    return pl.pallas_call(
        kernel,
        name=name,
        out_shape=out_shape,
        in_specs=in_specs,
        out_specs=out_specs or jax.tree.map(lambda _: VMEM, out_shape),
        scratch_shapes=scratch,
        compiler_params=pltpu.CompilerParams(vmem_limit_bytes=16 << 20),
    )


def shaped(shape, dtype):
    return jax.ShapeDtypeStruct(shape, dtype)


def in_hbm(array):
    return pltpu.with_memory_space_constraint(array, pltpu.HBM)


def mm(a, b, precision=None):
    return lax.dot_general(
        a, b, (((1,), (0,)), ((), ())), preferred_element_type=F32, precision=precision
    )


def mm_nt(a, b, precision=None):
    return lax.dot_general(
        a, b, (((1,), (1,)), ((), ())), preferred_element_type=F32, precision=precision
    )


def split(a):
    high = a.astype(BF16)
    return high, (a - high.astype(F32)).astype(BF16)


def iota(shape, dim):
    return lax.broadcasted_iota(jnp.int32, shape, dim)


def spread_kernel(w_hbm, out_hbm, w_ref, out_ref, sems):
    fetch = pltpu.make_async_copy(w_hbm, w_ref, sems.at[0])
    fetch.start()
    fetch.wait()
    out_ref[...] = jnp.broadcast_to(w_ref[...][None], out_ref.shape)
    store = pltpu.make_async_copy(out_ref, out_hbm, sems.at[1])
    store.start()
    store.wait()


def prelude_kernel(x_hbm, grad_hbm, dt_hbm, decay_hbm, hidden_hbm,
                   pair_ref, scaled_hbm, scaled_t_ref, running_t_ref, hidden_t_hbm,
                   x_ref, grad_ref, dt_t_ref, decay_t_ref, hidden_ref, scaled_ref, hidden_t_ref,
                   in_sems, x_sems, grad_sems, out_sems, *, parts):
    heads, rows = dt_t_ref.shape
    size = x_ref.shape[1] // heads
    groups = x_sems.shape[0]
    wide = x_ref.shape[1] // groups
    small = [
        pltpu.make_async_copy(source, target, in_sems.at[k])
        for k, (source, target) in enumerate(
            ((decay_hbm, decay_t_ref), (dt_hbm, dt_t_ref), (hidden_hbm, hidden_ref))
        )
    ]

    def columns(source, target, sems, group):
        lanes = pl.ds(group * wide, wide)
        return pltpu.make_async_copy(source.at[:, lanes], target.at[:, lanes], sems.at[group])

    x_in = [columns(x_hbm, x_ref, x_sems, group) for group in range(groups)]
    grad_in = [columns(grad_hbm, grad_ref, grad_sems, group) for group in range(groups)]
    scaled_out = [columns(scaled_ref, scaled_hbm, out_sems, group) for group in range(groups)]
    hidden_out = pltpu.make_async_copy(hidden_t_ref, hidden_t_hbm, in_sems.at[3])
    for copy in small[:2]:
        copy.start()
    for group in range(groups):
        x_in[group].start()
        grad_in[group].start()
    small[2].start()
    for copy in small[:2]:
        copy.wait()
    causal = iota((rows, rows), 0) >= iota((rows, rows), 1)
    upto = iota((rows, rows), 0) <= iota((rows, rows), 1)
    running_t = mm(decay_t_ref[...], upto.astype(F32), HIGH)
    running_t_ref[...] = running_t
    running = running_t.T
    dt_t = dt_t_ref[...]
    to_end_t = dt_t * jnp.exp(running_t[:, rows - 1 : rows] - running_t)
    to_end = to_end_t.T
    from_start_t = jnp.exp(running_t)
    from_start = jnp.exp(running)
    first = iota((rows, 2 * size), 1) < size
    total = jnp.zeros((rows, rows), F32)
    for pair in range(heads // 2):
        group = 2 * size * pair // wide
        if 2 * size * pair % wide == 0:
            x_in[group].wait()
            grad_in[group].wait()
        lanes = slice(2 * size * pair, 2 * size * (pair + 1))
        even, odd = 2 * pair, 2 * pair + 1
        x = x_ref[:, lanes]
        grad = grad_ref[:, lanes]
        zero = jnp.zeros_like(grad)
        both = jnp.concatenate([jnp.where(first, grad, zero), jnp.where(first, zero, grad)], axis=0)
        products = mm_nt(both, x)
        for place, head in enumerate((even, odd)):
            spread = running[:, head : head + 1] - running_t[head : head + 1, :]
            segment = jnp.exp(jnp.where(causal, spread, NEG))
            part = products[place * rows : (place + 1) * rows, :]
            total = total + segment * (part * dt_t[head : head + 1, :])
        x = x.astype(F32)
        grad = grad.astype(F32)
        x_scale = jnp.where(first, to_end[:, even : even + 1], to_end[:, odd : odd + 1])
        grad_scale = jnp.where(first, from_start[:, even : even + 1], from_start[:, odd : odd + 1])
        x_high, x_low = split(x * x_scale)
        grad_high, grad_low = split(grad * grad_scale)
        for k, value in enumerate((x_high, grad_high, x_low, grad_low)):
            scaled_ref[k * rows : (k + 1) * rows, lanes] = value
        x_t = x.T
        grad_t = grad.T
        for place, head in enumerate((even, odd)):
            here = slice(place * size, (place + 1) * size)
            there = slice(size * head, size * (head + 1))
            x_high, x_low = split(x_t[here, :] * to_end_t[head : head + 1, :])
            grad_high, grad_low = split(grad_t[here, :] * from_start_t[head : head + 1, :])
            for k, value in enumerate((x_high, grad_high, x_low, grad_low)):
                scaled_t_ref[there, k * rows : (k + 1) * rows] = value
        if 2 * size * (pair + 1) % wide == 0:
            scaled_out[group].start()
    pair_ref[...] = total
    small[2].wait()
    if parts:
        count = hidden_ref.shape[1] // parts
        for k in range(0, hidden_ref.shape[1], 128):
            block = hidden_ref[:, k : k + 128].astype(F32).T.astype(BF16)
            for r in range(0, 128, parts):
                piece = (k + r) // parts
                target = ((piece % 2) * (count // 2) + piece // 2) * parts
                hidden_t_ref[target : target + parts, :] = block[r : r + parts, :]
    else:
        hidden_t_ref[...] = jnp.zeros_like(hidden_t_ref)
    hidden_out.start()
    for copy in scaled_out:
        copy.wait()
    hidden_out.wait()


def states_kernel(place_ref, hidden_ref, w_ref, scaled_t_ref, running_t_ref,
                  projected_ref, keep_ref, send_ref, totals_ref):
    rows, width = projected_ref.shape
    heads = running_t_ref.shape[0]
    half = scaled_t_ref.shape[0] // 2
    projected = mm(hidden_ref[...], w_ref[...].reshape(hidden_ref.shape[1], width))
    projected_ref[...] = projected
    first = iota(projected.shape, 1) < width // 2
    blocks = jnp.concatenate(
        [jnp.where(first, projected, 0.0), jnp.where(first, 0.0, projected)], axis=0
    )
    high, low = split(blocks)
    twice = jnp.concatenate([high, high], axis=0)
    totals_ref[...] = jnp.broadcast_to(running_t_ref[:, rows - 1 : rows], (heads, width))
    mine = place_ref[0]
    for which, out_ref in ((1 - mine, send_ref), (mine, keep_ref)):
        scaled = scaled_t_ref[pl.ds(pl.multiple_of(which * half, half), half), :]
        out_ref[0:half, :] = mm(scaled, twice) + mm(scaled[:, 0 : 2 * rows], low)
        out_ref[half:, :] = totals_ref[
            pl.ds(pl.multiple_of(which * (heads // 2), heads // 2), heads // 2), :
        ]


def chip_kernel(place_ref, keep_ref, recv_ref, out_ref, *, size):
    core = place_ref[0]
    chips, chunk, width = out_ref.shape
    rows = chunk - 8
    half = chips * rows
    first_lanes = iota((rows, width), 1) < width // 2
    term = iota((8, width), 0)
    for k in range(chips):
        head = k * rows // size
        here = slice(k * rows, (k + 1) * rows)
        total = slice(half + head, half + head + 1)
        keep = keep_ref[here, :]
        recv = recv_ref[here, :]
        total_kept, total_received = keep_ref[total, :], recv_ref[total, :]
        over_kept, over_received = jnp.exp(total_kept), jnp.exp(total_received)
        as_first = jnp.where(first_lanes, keep * over_received + recv, keep + over_kept * recv)
        as_second = jnp.where(first_lanes, recv * over_kept + keep, recv + over_received * keep)
        out_ref[k, 0:rows, :] = jnp.where(core == 0, as_first, as_second).astype(BF16)
        over = jnp.exp(total_kept + total_received)
        high = over.astype(BF16).astype(F32)
        middle, low = split(over - high)
        terms = jnp.where(term == 0, high, jnp.where(term == 1, middle.astype(F32), low.astype(F32)))
        out_ref[k, rows:, :] = terms.astype(BF16)


def scan_kernel(in_ref, out_ref, before_ref):
    chips, rows, width = out_ref.shape
    first_lanes = iota((rows, width), 1) < width // 2

    def step(k, carried):
        terms = in_ref[k, rows:, :].astype(F32)
        over = terms[0:1, :] + terms[1:2, :] + terms[2:3, :]
        return over * carried + in_ref[k, 0:rows, :].astype(F32)

    def forward(k, carried):
        before_ref[k] = carried
        return step(k, carried)

    def backward(count, carried):
        k = chips - 1 - count
        out_ref[k] = jnp.where(first_lanes, before_ref[k], carried).astype(BF16)
        return step(k, carried)

    start = jnp.zeros((rows, width), F32)
    lax.fori_loop(0, chips, forward, start, unroll=chips <= 16)
    lax.fori_loop(0, chips, backward, start, unroll=chips <= 16)


def core_kernel(place_ref, in_ref, keep_ref, recv_ref, mine_ref, send_ref, *, size):
    core = place_ref[0]
    half, width = in_ref.shape
    plain = iota((size, width), 1) // (width // 2) == core
    for k in range(half // size):
        here = slice(k * size, (k + 1) * size)
        total = slice(half + k, half + k + 1)
        keep = keep_ref[here, :]
        recv = recv_ref[here, :]
        arrived = in_ref[here, :].astype(F32)
        for_mine = recv + jnp.exp(recv_ref[total, :]) * arrived
        for_other = keep + jnp.exp(keep_ref[total, :]) * arrived
        mine_ref[here, :] = jnp.where(plain, arrived, for_mine)
        send_ref[here, :] = jnp.where(plain, for_other, arrived)


def inside_kernel(projected_ref, pair_ref, grad_ref, running_t_ref, d_in_ref, d_proj_ref):
    heads, rows = running_t_ref.shape
    width = projected_ref.shape[1]
    size = grad_ref.shape[1] // heads
    projected = projected_ref[...]
    swapped = pltpu.roll(projected, width // 2, 1)
    first = iota(projected.shape, 1) < width // 2
    scores_t = mm_nt(jnp.where(first, projected, 0.0), swapped, HIGH)
    running_t = running_t_ref[...]
    running = running_t.T
    later = iota((rows, rows), 1) >= iota((rows, rows), 0)
    lanes_first = iota((rows, 2 * size), 1) < size
    for pair in range(heads // 2):
        lanes = slice(2 * size * pair, 2 * size * (pair + 1))
        grad = grad_ref[:, lanes]
        zero = jnp.zeros_like(grad)
        both = jnp.concatenate(
            [jnp.where(lanes_first, grad, zero), jnp.where(lanes_first, zero, grad)], axis=0
        )
        highs, lows = [], []
        for head in (2 * pair, 2 * pair + 1):
            spread = running_t[head : head + 1, :] - running[:, head : head + 1]
            high, low = split(jnp.exp(jnp.where(later, spread, NEG)) * scores_t)
            highs.append(high)
            lows.append(low)
        d_in_ref[:, lanes] = mm(jnp.concatenate(highs, axis=1), both) + mm(
            jnp.concatenate(lows, axis=1), both
        )
    pair_sum = pair_ref[...]
    onto_c = mm(pair_sum, projected, HIGH)
    onto_b = mm(pair_sum.T, projected, HIGH)
    d_proj_ref[...] = pltpu.roll(jnp.where(first, onto_c, onto_b), width // 2, 1)


def project_kernel(place_ref, mine_ref, recv_ref, scaled_ref, d_proj_ref, hidden_t_ref,
                   d_low_ref, keep_ref, send_ref, high_ref, low_ref):
    rows, width = d_proj_ref.shape
    half = mine_ref.shape[0]
    core = place_ref[0]
    for which, in_ref in ((core, mine_ref), (1 - core, recv_ref)):
        there = pl.ds(pl.multiple_of(which * half, half), half)
        high, low = split(in_ref[...])
        high_ref[there, :] = high
        low_ref[there, :] = low
    by_high = mm(scaled_ref[...], high_ref[...])
    by_low = mm(scaled_ref[0 : 2 * rows, :], low_ref[...])
    onto = by_high[0 : 2 * rows, :] + by_high[2 * rows :, :] + by_low
    first = iota((rows, width), 1) < width // 2
    crossing = jnp.where(first, onto[rows:, :], onto[:rows, :])
    d_low = (d_proj_ref[...] + pltpu.roll(crossing, width // 2, 1)).astype(BF16)
    d_low_ref[...] = d_low
    part = send_ref.shape[0]
    for which, out_ref in ((1 - core, send_ref), (core, keep_ref)):
        out_ref[...] = mm(hidden_t_ref[pl.ds(pl.multiple_of(which * part, part), part), :], d_low)


def inputs_kernel(place_ref, mine_ref, recv_ref, projected_ref, d_in_ref, dt_t_ref, running_t_ref,
                  d_low_ref, w_ref, grad_x_ref, grad_hidden_ref, entries_ref):
    half = mine_ref.shape[0]
    core = place_ref[0]
    for which, in_ref in ((core, mine_ref), (1 - core, recv_ref)):
        there = pl.ds(pl.multiple_of(which * half, half), half)
        entries_ref[there, :] = in_ref[...].astype(BF16)
    heads, rows = dt_t_ref.shape
    width = projected_ref.shape[1]
    size = d_in_ref.shape[1] // heads
    grad_hidden_ref[...] = mm_nt(
        d_low_ref[...], w_ref[...].reshape(grad_hidden_ref.shape[1], width)
    )
    swapped = pltpu.roll(projected_ref[...], width // 2, 1)
    first = iota((rows, width), 1) < width // 2
    b_high, b_low = split(jnp.where(first, 0.0, swapped))
    b_both = jnp.concatenate([b_high, b_low], axis=0)
    running_t = running_t_ref[...]
    dt = dt_t_ref[...].T
    to_end = jnp.exp(running_t[:, rows - 1 : rows] - running_t).T
    lanes_first = iota((rows, 2 * size), 1) < size
    for pair in range(heads // 2):
        lanes = slice(2 * size * pair, 2 * size * (pair + 1))
        even, odd = 2 * pair, 2 * pair + 1
        crossing = mm_nt(b_both, entries_ref[lanes, :])
        crossing = crossing[:rows, :] + crossing[rows:, :]
        decay = jnp.where(lanes_first, to_end[:, even : even + 1], to_end[:, odd : odd + 1])
        step = jnp.where(lanes_first, dt[:, even : even + 1], dt[:, odd : odd + 1])
        grad_x_ref[:, lanes] = step * (d_in_ref[:, lanes] + decay * crossing)


def sum_kernel(terms_ref, out_ref, *, scale):
    out_ref[...] = jnp.sum(terms_ref[...], axis=0) * scale


def per_device(hidden, x_act, dt_step, log_decay, w_bc, grad_y):
    devices = lax.axis_size("outer") * lax.axis_size("inner")
    rows, model = hidden.shape
    heads = dt_step.shape[1]
    flat = x_act.shape[1]
    size = flat // heads
    w_rows, width = w_bc.shape
    half = flat // 2
    chips = devices // 2
    slice_rows = half // chips
    position = lax.axis_index("outer") * lax.axis_size("inner") + lax.axis_index("inner")
    place = (position & 1).astype(jnp.int32).reshape(1)
    partner = [(i, i ^ 1) for i in range(devices)]
    same_core = [list(range(core, devices, 2)) for core in range(2)]

    def exchange(array):
        return lax.all_to_all(
            array, AXES, split_axis=0, concat_axis=0, tiled=True, axis_index_groups=same_core
        )

    spread = call(
        spread_kernel, "spread", pltpu.HBM((devices, w_rows, width), BF16), [HBM],
        [pltpu.VMEM((w_rows, width), BF16), pltpu.VMEM((devices, w_rows, width), BF16),
         pltpu.SemaphoreType.DMA((2,))],
        HBM,
    )(in_hbm(w_bc))
    gathered = lax.all_to_all(spread, AXES, split_axis=0, concat_axis=0, tiled=True)
    dt_t = dt_step.T
    in_kernel = w_rows % 16 == 0
    hidden_t_rows = model if in_kernel else 16
    groups = 4
    pair_sum, scaled, scaled_t, running_t, hidden_t = call(
        functools.partial(prelude_kernel, parts=w_rows if in_kernel else 0), "prelude",
        (shaped((rows, rows), F32), pltpu.HBM((4 * rows, flat), BF16), shaped((flat, 4 * rows), BF16),
         shaped((heads, rows), F32), pltpu.HBM((hidden_t_rows, rows), BF16)),
        [HBM] * 5,
        [pltpu.VMEM((rows, flat), BF16), pltpu.VMEM((rows, flat), BF16),
         pltpu.VMEM((heads, rows), F32), pltpu.VMEM((heads, rows), F32),
         pltpu.VMEM((rows, model), BF16), pltpu.VMEM((4 * rows, flat), BF16),
         pltpu.VMEM((hidden_t_rows, rows), BF16)]
        + [pltpu.SemaphoreType.DMA((groups,)) for _ in range(4)],
        (VMEM, HBM, VMEM, VMEM, HBM),
    )(in_hbm(x_act), in_hbm(grad_y), in_hbm(dt_t), in_hbm(log_decay.T), in_hbm(hidden))
    weights = gathered
    if not in_kernel:
        weights = gathered.reshape(model, width)
        hidden_t = hidden.T.reshape(chips, 2, w_rows, rows).transpose(1, 0, 2, 3)
        hidden_t = hidden_t.reshape(model, rows)
    extended = half + heads // 2
    projected, keep, send, _ = call(
        states_kernel, "states",
        (shaped((rows, width), F32), shaped((extended, width), F32), shaped((extended, width), F32),
         shaped((heads, width), F32)),
        [SMEM] + [VMEM] * 4,
    )(place, hidden, weights, scaled_t, running_t)
    recv = lax.ppermute(send, AXES, partner)
    chip_total = call(
        functools.partial(chip_kernel, size=size), "chip",
        shaped((chips, slice_rows + 8, width), BF16), [SMEM, VMEM, VMEM],
    )(place, keep, recv)
    slices = exchange(chip_total)
    d_in, d_proj = call(
        inside_kernel, "inside", (shaped((rows, flat), F32), shaped((rows, width), F32)),
        [VMEM] * 4,
    )(projected, pair_sum, grad_y, running_t)
    around = call(
        scan_kernel, "scan", shaped((chips, slice_rows, width), BF16), [VMEM],
        [pltpu.VMEM((chips, slice_rows, width), F32)],
    )(slices)
    arrived = exchange(around).reshape(half, width)
    mine, send_back = call(
        functools.partial(core_kernel, size=size), "core",
        (shaped((half, width), F32), shaped((half, width), F32)),
        [SMEM, VMEM, VMEM, VMEM],
    )(place, arrived, keep, recv)
    recv_back = lax.ppermute(send_back, AXES, partner)
    d_low, keep_term, send_term = call(
        project_kernel, "project",
        (shaped((rows, width), BF16), shaped((model // 2, width), F32),
         shaped((model // 2, width), F32)),
        [SMEM] + [VMEM] * 5,
        [pltpu.VMEM((flat, width), BF16), pltpu.VMEM((flat, width), BF16)],
    )(place, mine, recv_back, scaled, d_proj, hidden_t)
    recv_term = lax.ppermute(send_term, AXES, partner)
    terms = exchange((keep_term + recv_term).reshape(chips, w_rows, width))
    grad_x, grad_hidden = call(
        inputs_kernel, "inputs", (shaped((rows, flat), F32), shaped((rows, model), F32)),
        [SMEM] + [VMEM] * 8, [pltpu.VMEM((flat, width), BF16)],
    )(place, mine, recv_back, projected, d_in, dt_t, running_t, d_low, weights)
    scale = 1.0 / math.sqrt(rows * devices)
    grad_proj = call(
        functools.partial(sum_kernel, scale=scale), "total", shaped((w_rows, width), F32), [VMEM]
    )(terms)
    return (grad_x, grad_hidden, grad_proj)


def solution(mesh):
    spec = P(AXES, None)
    return jax.shard_map(
        per_device, mesh=mesh, in_specs=(spec,) * 6, out_specs=(spec,) * 3, check_vma=False
    )
```

time: 384 us -> 72.1 us (0.19)
  waiting for transfers between devices: 198 us -> 17.2 us
  local copies, waits for them, and re-layouts: 44.6 us -> 0.02 us
  blocking collectives: 61.5 us -> 27 us
  other arithmetic: 34 us -> 0.73 us
  matrix products: 17.4 us -> 0 us
  Pallas kernels: 0 us -> 14.7 us
  between operations: 14.8 us -> 0.75 us
    unnamed x4 -> x0, waiting for transfers between devices: 131 us -> none
    all_gather x2 -> x0, waiting for transfers between devices: 46.3 us -> none  [carried_in(): everything = jax.tree.map(lambda part: lax.all_gather(part, axis), array)]
    all_gather x1 -> x0, blocking collectives: 44.2 us -> none  [per_device(): weights_full = lax.all_gather(w_bc, ('outer', 'inner'), axis=0, tiled=True)]
    all_to_all x0 -> x2, blocking collectives: none -> 27 us  [exchange(): lax.all_to_all(array, AXES, split_axis=0, concat_axis=0, tiled=True, axis...]
    unnamed x45 -> x10, local copies, waits for them, and re-layouts: 25 us -> 0.02 us
    dot_general x13 -> x0, matrix products: 17.4 us -> none  [the longest x2 5.95 us: block_step(): jnp.einsum('hij,jhp->ihp', segment * scores[None], inputs, precision=HIGH)]
    unnamed x1 -> x0, blocking collectives: 17.3 us -> none
    select_n x16 -> x0, other arithmetic: 15.9 us -> none  [step(): return jax.tree.map(lambda a, b: jnp.where(reached, a, b), new, before)]
  transfers between devices with their start and end apart: 6 -> 5, of which waited for: 5 -> 5; matrix products, arithmetic and copies ran while one was open for 11% -> 0% of each run, Pallas kernels for 0% -> 12%
where the time goes in v1:
time: 72.1 us; the launch traced here: 71.6 us
  blocking collectives  27 us (37%)
  waiting for transfers between devices  17.2 us (24%)
  Pallas kernels  14.7 us (20%)
  starting transfers between devices  11.2 us (16%)
  between operations  0.75 us (1%)
  other arithmetic  0.73 us (1%)
    all_to_all x2, blocking collectives, exchange(): lax.all_to_all(array, AXES, split_axis=0, concat_axis=0, tiled=True, axis...  27 us
    all_to_all x1, waiting for transfers between devices, exchange(): lax.all_to_all(array, AXES, split_axis=0, concat_axis=0, tiled=True, axis...  7.95 us
    all_to_all x1, starting transfers between devices, per_device(): lax.all_to_all(spread, AXES, split_axis=0, concat_axis=0, tiled=True)  7.33 us
    all_to_all x1, waiting for transfers between devices, per_device(): lax.all_to_all(spread, AXES, split_axis=0, concat_axis=0, tiled=True)  5.68 us
    pallas_call x1, Pallas kernels, per_device(): call(functools.partial(prelude_kernel, parts=w_rows if in_kernel else 0),...  4.88 us
    all_to_all x1, starting transfers between devices, exchange(): lax.all_to_all(array, AXES, split_axis=0, concat_axis=0, tiled=True, axis...  3.55 us
    pallas_call x1, Pallas kernels, per_device(): call(inputs_kernel, 'inputs', (shaped((rows, flat), F32), shaped((rows, m...  2.47 us
    ppermute x1, waiting for transfers between devices, per_device(): recv = lax.ppermute(send, AXES, partner)  1.92 us
  transfers between devices with their start and end apart: 5, of which 5 were waited for; matrix products, arithmetic and copies ran while one was open for 0% of the time, Pallas kernels for 12%

profile of v1, /device:TPU:0, one launch (start us, length us, event | category | flops | bytes accessed | tf_op | source)
XLA Modules:
  0.0 71.6 jit_solution(10198908833301898102)
XLA Ops:
  0.6 0.0 copy-start.2
  0.6 1.5 %spread.1 = bf16[32,32,128]{2,1,0:T(8,128)(2,1)} custom-call(bf16[32,128]{1,0:T(8,128)(2,1)} %w_hbm.1), custom_call_target="tpu_custom_call" | custom-call | tf_op jit(solution)/shard_map/spread/pallas_call | solution.py:367
  2.1 7.3 %all-to-all-start = ((bf16[32,32,128]{2,1,0:T(8,128)(2,1)}), bf16[32,32,128]{2,1,0:T(8,128)(2,1)S(1)}, u32[]{:S(2)}, u32[]{:S(2)}) async-start(bf16[32,32,128]{2,1,0:T(8,128)(2,1)} %spread.1), calls=%async_computation | async-start | bytes 524288 | tf_op jit(solution)/shard_map/all_to_all | solution.py:373
  9.5 4.9 %prelude.1 = (f32[128,128]{1,0:T(8,128)S(1)}, bf16[512,2048]{1,0:T(8,128)(2,1)}, bf16[2048,512]{1,0:T(8,128)(2,1)S(1)}, f32[32,128]{1,0:T(8,128)S(1)}, bf16[1024,128]{1,0:T(8,128)(2,1)}) custom-call(bf16[128,2048]{1,0:T(8,128)(2,1)} %x_hbm.1, bf16[128,2048]{1,0:T(8,128)(2,1)} %grad_ref.1, f32[32,128]{1,0:T(8,128)} %bitcast.6, f32[32,128]{1,0:T(8,128)} %bitcast.8, ...), custom_call_target="tpu_custom_call" | custom-call | tf_op jit(solution)/shard_map/prelude/pallas_call | solution.py:378
  14.4 5.7 %all-to-all-done.w_ref = bf16[32,32,128]{2,1,0:T(8,128)(2,1)S(1)} async-done(((bf16[32,32,128]{2,1,0:T(8,128)(2,1)}), bf16[32,32,128]{2,1,0:T(8,128)(2,1)S(1)}, u32[]{:S(2)}, u32[]{:S(2)}) %all-to-all-start) | async-done | bytes 262176 | tf_op jit(solution)/shard_map/all_to_all | solution.py:373
  20.1 0.0 copy-done.2
  20.1 1.7 %states.1 = (f32[128,128]{1,0:T(8,128)S(1)}, f32[1040,128]{1,0:T(8,128)S(1)}, f32[1040,128]{1,0:T(8,128)S(1)}, f32[32,128]{1,0:T(8,128)}) custom-call(s32[1]{0:T(128)} %bitcast.place_ref, bf16[128,1024]{1,0:T(8,128)(2,1)S(1)} %copy-done.2, bf16[32,32,128]{2,1,0:T(8,128)(2,1)S(1)} %all-to-all-done.w_ref, ...), custom_call_target="tpu_custom_call" | custom-call | tf_op jit(solution)/shard_map/states/pallas_call | solution.py:396
  21.8 0.0 collective-permute-start
  21.8 1.9 %collective-permute-done.recv_ref = f32[1040,128]{1,0:T(8,128)S(1)} collective-permute-done((f32[1040,128]{1,0:T(8,128)S(1)}, f32[1040,128]{1,0:T(8,128)S(1)}, u32[]{:S(2)}, u32[]{:S(2)}) %collective-permute-start) | collective-permute-done | bytes 532512 | tf_op jit(solution)/shard_map/ppermute | solution.py:402
  23.7 0.0 copy-start.1
  23.7 0.2 chip.1
  23.9 0.0 copy-start
  23.9 0.0 copy-start.3
  23.9 14.3 %all_to_all.20.in_ref = bf16[16,72,128]{2,1,0:T(8,128)(2,1)S(1)} all-to-all(bf16[16,72,128]{2,1,0:T(8,128)(2,1)S(1)} %chip.1), channel_id=1, replica_groups={{0,2,4,6,8,10,12,14,16,18,20,22,24,26,28,30},{1,3,5,7,9,11,13,15,17,19,..., dimensions={0} | all-to-all | bytes 589824 | tf_op jit(solution)/shard_map/all_to_all | solution.py:363
  38.2 0.1 scan.1
  38.4 12.7 %all_to_all.21 = bf16[16,64,128]{2,1,0:T(8,128)(2,1)S(1)} all-to-all(bf16[16,64,128]{2,1,0:T(8,128)(2,1)S(1)} %scan.1), channel_id=1, replica_groups={{0,2,4,6,8,10,12,14,16,18,20,22,24,26,28,30},{1,3,5,7,9,11,13,15,17,19,..., dimensions={0} | all-to-all | bytes 524288 | tf_op jit(solution)/shard_map/all_to_all | solution.py:363
  51.1 0.2 core.1
  51.2 0.1 collective-permute-start.1
  51.3 0.0 copy-done.1
  51.3 1.5 %inside.1 = (f32[128,2048]{1,0:T(8,128)S(1)}, f32[128,128]{1,0:T(8,128)S(1)}) custom-call(f32[128,128]{1,0:T(8,128)S(1)} %get-tuple-element.26.projected_ref, f32[128,128]{1,0:T(8,128)S(1)} %get-tuple-element.27.pair_ref, bf16[128,2048]{1,0:T(8,128)(2,1)S(1)} %copy-done.1, f32[32,128]{1,0:T(8,128)S(1)} %get-tuple-element.21.running_t_ref), custom_call_target="tpu_custom_call" | custom-call | tf_op jit(solution)/shard_map/inside/pallas_call | solution.py:408
  52.9 0.3 collective-permute-done.1.recv_ref
  53.2 0.0 copy-done
  53.2 0.0 copy-done.3
  53.2 0.0 copy-start.4
  53.2 1.4 %project.1 = (bf16[128,128]{1,0:T(8,128)(2,1)S(1)}, f32[512,128]{1,0:T(8,128)S(1)}, f32[512,128]{1,0:T(8,128)S(1)}) custom-call(s32[1]{0:T(128)} %bitcast.place_ref, f32[1024,128]{1,0:T(8,128)S(1)} %get-tuple-element.24.mine_ref, f32[1024,128]{1,0:T(8,128)S(1)} %collective-permute-done.1.recv_ref, bf16[512,2048]{1,0:T(8,128)(2,1)S(1)} %copy-done, ...), custom_call_target="tpu_custom_call" | custom-call | tf_op jit(solution)/shard_map/project/pallas_call | solution.py:423
  54.7 0.3 collective-permute-start.2
  54.9 1.3 %collective-permute-done.2 = f32[512,128]{1,0:T(8,128)S(1)} collective-permute-done((f32[512,128]{1,0:T(8,128)S(1)}, f32[512,128]{1,0:T(8,128)S(1)}, u32[]{:S(2)}, u32[]{:S(2)}) %collective-permute-start.2) | collective-permute-done | bytes 262176 | tf_op jit(solution)/shard_map/ppermute | solution.py:430
  56.3 0.7 %add.7 = f32[512,128]{1,0:T(8,128)} add(f32[512,128]{1,0:T(8,128)S(1)} %get-tuple-element.35, f32[512,128]{1,0:T(8,128)S(1)} %collective-permute-done.2) | non-fusion elementwise | flops 65536 | bytes 786432 | tf_op jit(solution)/shard_map/add | solution.py:431
  57.0 3.5 %all-to-all-start.3 = ((f32[16,32,128]{2,1,0:T(8,128)}), f32[16,32,128]{2,1,0:T(8,128)S(1)}, u32[]{:S(2)}, u32[]{:S(2)}) async-start(f32[16,32,128]{2,1,0:T(8,128)} %bitcast.4), calls=%async_computation.3 | async-start | bytes 524288 | tf_op jit(solution)/shard_map/all_to_all | solution.py:363
  60.5 0.0 copy-done.4
  60.6 2.5 %inputs.1 = (f32[128,2048]{1,0:T(8,128)}, f32[128,1024]{1,0:T(8,128)}) custom-call(s32[1]{0:T(128)} %bitcast.place_ref, f32[1024,128]{1,0:T(8,128)S(1)} %get-tuple-element.24.mine_ref, f32[1024,128]{1,0:T(8,128)S(1)} %collective-permute-done.1.recv_ref, f32[128,128]{1,0:T(8,128)S(1)} %get-tuple-element.26.projected_ref, ...), custom_call_target="tpu_custom_call" | custom-call | tf_op jit(solution)/shard_map/inputs/pallas_call | solution.py:432
  63.0 7.9 %all-to-all-done.3.terms_ref = f32[16,32,128]{2,1,0:T(8,128)S(1)} async-done(((f32[16,32,128]{2,1,0:T(8,128)}), f32[16,32,128]{2,1,0:T(8,128)S(1)}, u32[]{:S(2)}, u32[]{:S(2)}) %all-to-all-start.3) | async-done | bytes 262176 | tf_op jit(solution)/shard_map/all_to_all | solution.py:363
  71.0 0.6 total.1
Async XLA Ops:
  0.6 19.4 %copy-start.2 = (bf16[128,1024]{1,0:T(8,128)(2,1)S(1)}, bf16[128,1024]{1,0:T(8,128)(2,1)}, u32[]{:S(2)}) copy-start(bf16[128,1024]{1,0:T(8,128)(2,1)} %hidden_ref.1) | copy-start | bytes 786436
  2.1 17.9 %all-to-all-start = ((bf16[32,32,128]{2,1,0:T(8,128)(2,1)}), bf16[32,32,128]{2,1,0:T(8,128)(2,1)S(1)}, u32[]{:S(2)}, u32[]{:S(2)}) async-start(bf16[32,32,128]{2,1,0:T(8,128)(2,1)} %spread.1), calls=%async_computation | async-start | bytes 524288 | tf_op jit(solution)/shard_map/all_to_all | solution.py:373
  21.8 1.9 %collective-permute-start = (f32[1040,128]{1,0:T(8,128)S(1)}, f32[1040,128]{1,0:T(8,128)S(1)}, u32[]{:S(2)}, u32[]{:S(2)}) collective-permute-start(f32[1040,128]{1,0:T(8,128)S(1)} %get-tuple-element.23), channel_id=1, source_target_pairs={{0,1},{1,0},{2,3},{3,2},{4,5},{5,4},{6,7},{7,6},{8,9},{9,8},{10,11... | collective-permute-start | bytes 1597448 | tf_op jit(solution)/shard_map/ppermute | solution.py:402
  23.7 27.6 %copy-start.1 = (bf16[128,2048]{1,0:T(8,128)(2,1)S(1)}, bf16[128,2048]{1,0:T(8,128)(2,1)}, u32[]{:S(2)}) copy-start(bf16[128,2048]{1,0:T(8,128)(2,1)} %grad_ref.1) | copy-start | bytes 1572868
  23.9 29.3 %copy-start = (bf16[512,2048]{1,0:T(8,128)(2,1)S(1)}, bf16[512,2048]{1,0:T(8,128)(2,1)}, u32[]{:S(2)}) copy-start(bf16[512,2048]{1,0:T(8,128)(2,1)} %get-tuple-element.29.scaled_ref) | copy-start | bytes 6291460
  23.9 29.3 %copy-start.3 = (bf16[1024,128]{1,0:T(8,128)(2,1)S(1)}, bf16[1024,128]{1,0:T(8,128)(2,1)}, u32[]{:S(2)}) copy-start(bf16[1024,128]{1,0:T(8,128)(2,1)} %get-tuple-element.31.hidden_t_ref) | copy-start | bytes 786436
  51.2 2.0 %collective-permute-start.1 = (f32[1024,128]{1,0:T(8,128)S(1)}, f32[1024,128]{1,0:T(8,128)S(1)}, u32[]{:S(2)}, u32[]{:S(2)}) collective-permute-start(f32[1024,128]{1,0:T(8,128)S(1)} %get-tuple-element.25), channel_id=1, source_target_pairs={{0,1},{1,0},{2,3},{3,2},{4,5},{5,4},{6,7},{7,6},{8,9},{9,8},{10,11... | collective-permute-start | bytes 1572872 | tf_op jit(solution)/shard_map/ppermute | solution.py:422
  53.2 7.3 %copy-start.4 = (f32[128,32]{0,1:T(8,128)S(1)}, f32[128,32]{0,1:T(8,128)}, u32[]{:S(2)}) copy-start(f32[128,32]{0,1:T(8,128)} %param.8) | copy-start | bytes 49156
  54.7 1.6 %collective-permute-start.2 = (f32[512,128]{1,0:T(8,128)S(1)}, f32[512,128]{1,0:T(8,128)S(1)}, u32[]{:S(2)}, u32[]{:S(2)}) collective-permute-start(f32[512,128]{1,0:T(8,128)S(1)} %get-tuple-element.36), channel_id=1, source_target_pairs={{0,1},{1,0},{2,3},{3,2},{4,5},{5,4},{6,7},{7,6},{8,9},{9,8},{10,11... | collective-permute-start | bytes 786440 | tf_op jit(solution)/shard_map/ppermute | solution.py:430
  57.0 14.0 %all-to-all-start.3 = ((f32[16,32,128]{2,1,0:T(8,128)}), f32[16,32,128]{2,1,0:T(8,128)S(1)}, u32[]{:S(2)}, u32[]{:S(2)}) async-start(f32[16,32,128]{2,1,0:T(8,128)} %bitcast.4), calls=%async_computation.3 | async-start | bytes 524288 | tf_op jit(solution)/shard_map/all_to_all | solution.py:363

commit v2 on v1

v2 whole, which is shorter than its diff:
```python
import functools
import math

import jax
import jax.numpy as jnp
from jax import lax
from jax.experimental import pallas as pl
from jax.experimental.pallas import tpu as pltpu
from jax.sharding import PartitionSpec as P


AXES = ("outer", "inner")
HIGH = lax.Precision.HIGHEST
F32 = jnp.float32
BF16 = jnp.bfloat16
NEG = -1e30
VMEM = pl.BlockSpec(memory_space=pltpu.MemorySpace.VMEM)
SMEM = pl.BlockSpec(memory_space=pltpu.MemorySpace.SMEM)
HBM = pl.BlockSpec(memory_space=pltpu.MemorySpace.HBM)


def call(kernel, out_shape, in_specs, scratch=(), out_specs=None):
    return pl.pallas_call(
        kernel,
        out_shape=out_shape,
        in_specs=in_specs,
        out_specs=out_specs or jax.tree.map(lambda _: VMEM, out_shape),
        scratch_shapes=scratch,
        compiler_params=pltpu.CompilerParams(vmem_limit_bytes=16 << 20),
    )


def shaped(shape, dtype):
    return jax.ShapeDtypeStruct(shape, dtype)


def in_hbm(array):
    return pltpu.with_memory_space_constraint(array, pltpu.HBM)


def mm(a, b, precision=None):
    return lax.dot_general(
        a, b, (((1,), (0,)), ((), ())), preferred_element_type=F32, precision=precision
    )


def mm_nt(a, b, precision=None):
    return lax.dot_general(
        a, b, (((1,), (1,)), ((), ())), preferred_element_type=F32, precision=precision
    )


def split(a):
    high = a.astype(BF16)
    return high, (a - high.astype(F32)).astype(BF16)


def iota(shape, dim):
    return lax.broadcasted_iota(jnp.int32, shape, dim)


def spread_kernel(w_hbm, dt_hbm, decay_hbm, out_hbm, small_ref, w_ref, out_ref, sems):
    fetches = [
        pltpu.make_async_copy(w_hbm, w_ref, sems.at[0]),
        pltpu.make_async_copy(dt_hbm, small_ref.at[0], sems.at[1]),
        pltpu.make_async_copy(decay_hbm, small_ref.at[1], sems.at[2]),
    ]
    for fetch in fetches:
        fetch.start()
    fetches[0].wait()
    out_ref[...] = jnp.broadcast_to(w_ref[...][None], out_ref.shape)
    store = pltpu.make_async_copy(out_ref, out_hbm, sems.at[3])
    store.start()
    for fetch in fetches[1:]:
        fetch.wait()
    store.wait()


def prelude_kernel(place_ref, x_hbm, x_other_hbm, grad_hbm, grad_other_hbm, small_ref,
                   small_other_ref, hidden_hbm, hidden_other_hbm,
                   pair_hbm, scaled_t_ref, running_t_ref, dt_t_hbm, hidden_ref,
                   hidden_t_hbm, x_both_hbm, grad_both_hbm,
                   x_ref, grad_ref, hidden_all_t_ref, hidden_t_ref, pair_ref,
                   dt_t_ref, x_sems, grad_sems, hidden_sems, out_sems, *, parts):
    core = place_ref[0]
    heads, rows = small_ref.shape[1] // 2, small_ref.shape[2]
    tokens = 2 * rows
    half = x_ref.shape[1]
    size = half // heads
    groups = x_sems.shape[1]
    wide = half // groups

    def fetch(sources, target, sems, group):
        copies = []
        for which, source in enumerate(sources):
            there = core if which == 0 else 1 - core
            start = pl.multiple_of(core * half + group * wide, wide)
            copies.append(pltpu.make_async_copy(
                source.at[:, pl.ds(start, wide)],
                target.at[pl.ds(pl.multiple_of(there * rows, rows), rows), pl.ds(group * wide, wide)],
                sems.at[which, group],
            ))
        return copies

    x_in = [fetch((x_hbm, x_other_hbm), x_ref, x_sems, group) for group in range(groups)]
    grad_in = [fetch((grad_hbm, grad_other_hbm), grad_ref, grad_sems, group) for group in range(groups)]
    hidden_in = [
        pltpu.make_async_copy(
            source, hidden_ref.at[pl.ds(pl.multiple_of(there * rows, rows), rows), :],
            hidden_sems.at[k],
        )
        for k, (source, there) in enumerate(((hidden_hbm, core), (hidden_other_hbm, 1 - core)))
    ]
    x_out = pltpu.make_async_copy(x_ref, x_both_hbm, out_sems.at[4])
    grad_out = pltpu.make_async_copy(grad_ref, grad_both_hbm, out_sems.at[0])
    hidden_out = pltpu.make_async_copy(hidden_t_ref, hidden_t_hbm, out_sems.at[1])
    pair_out = pltpu.make_async_copy(pair_ref, pair_hbm, out_sems.at[2])
    dt_out = pltpu.make_async_copy(dt_t_ref, dt_t_hbm, out_sems.at[3])
    for group in range(groups):
        for copy in x_in[group] + grad_in[group]:
            copy.start()
    for copy in hidden_in:
        copy.start()

    mine = pl.ds(pl.multiple_of(core * heads, heads), heads)

    def both_cores(index):
        own, other = small_ref[index, mine, :], small_other_ref[index, mine, :]
        return jnp.concatenate(
            [jnp.where(core == 0, own, other), jnp.where(core == 0, other, own)], axis=1
        )

    dt_t, decay_t = both_cores(0), both_cores(1)
    dt_t_ref[...] = dt_t
    dt_out.start()
    upto = iota((tokens, tokens), 0) <= iota((tokens, tokens), 1)
    running_t = mm(decay_t, upto.astype(F32), HIGH)
    running_t_ref[...] = running_t
    running = running_t.T
    to_end_t = dt_t * jnp.exp(running_t[:, tokens - 1 : tokens] - running_t)
    from_start_t = jnp.exp(running_t)
    causal = iota((rows, rows), 0) >= iota((rows, rows), 1)
    first = iota((tokens, 2 * size), 1) < size
    pair_ref[...] = jnp.zeros_like(pair_ref)
    for pair in range(heads // 2):
        group = 2 * size * pair // wide
        if 2 * size * pair % wide == 0:
            for copy in x_in[group] + grad_in[group]:
                copy.wait()
        lanes = slice(2 * size * pair, 2 * size * (pair + 1))
        even, odd = 2 * pair, 2 * pair + 1
        x = x_ref[:, lanes]
        grad = grad_ref[:, lanes]
        zero = jnp.zeros_like(grad)
        both = jnp.concatenate([jnp.where(first, grad, zero), jnp.where(first, zero, grad)], axis=0)
        products = mm_nt(both, x)
        for at, to in ((0, 0), (1, 0), (1, 1)):
            here, there = slice(at * rows, (at + 1) * rows), slice(to * rows, (to + 1) * rows)
            total = pair_ref[here, there]
            for place, head in enumerate((even, odd)):
                spread = running[here, head : head + 1] - running_t[head : head + 1, there]
                if at == to:
                    spread = jnp.where(causal, spread, NEG)
                start = place * tokens + at * rows
                part = products[start : start + rows, there]
                total = total + jnp.exp(spread) * (part * dt_t[head : head + 1, there])
            pair_ref[here, there] = total
        x_t = x.astype(F32).T
        grad_t = grad.astype(F32).T
        for place, head in enumerate((even, odd)):
            here = slice(place * size, (place + 1) * size)
            there = slice(size * head, size * (head + 1))
            x_high, x_low = split(x_t[here, :] * to_end_t[head : head + 1, :])
            grad_high, grad_low = split(grad_t[here, :] * from_start_t[head : head + 1, :])
            for k, value in enumerate((x_high, grad_high, x_low, grad_low)):
                scaled_t_ref[there, k * tokens : (k + 1) * tokens] = value
    x_out.start()
    grad_out.start()
    pair_out.start()
    for copy in hidden_in:
        copy.wait()
    if parts:
        for k in range(0, hidden_ref.shape[1], 128):
            block = hidden_ref[:, k : k + 128].astype(F32).T
            hidden_all_t_ref[k : k + 128, :] = block.astype(BF16)
        for k in range(hidden_t_ref.shape[0] // parts):
            start = pl.multiple_of((2 * k + core) * parts, parts)
            hidden_t_ref[k * parts : (k + 1) * parts, :] = hidden_all_t_ref[pl.ds(start, parts), :]
    else:
        hidden_t_ref[...] = jnp.zeros_like(hidden_t_ref)
    hidden_out.start()
    for copy in (x_out, grad_out, hidden_out, pair_out, dt_out):
        copy.wait()


def states_kernel(hidden_ref, w_ref, scaled_t_ref, running_t_ref, projected_ref, slices_ref):
    tokens, width = projected_ref.shape
    heads = running_t_ref.shape[0]
    chips, rows = slices_ref.shape[0], slices_ref.shape[1] - 8
    projected = mm(hidden_ref[...], w_ref[...].reshape(hidden_ref.shape[1], width))
    projected_ref[...] = projected
    first = iota(projected.shape, 1) < width // 2
    blocks = jnp.concatenate(
        [jnp.where(first, projected, 0.0), jnp.where(first, 0.0, projected)], axis=0
    )
    high, low = split(blocks)
    states = mm(scaled_t_ref[...], jnp.concatenate([high, high], axis=0))
    states = states + mm(scaled_t_ref[:, 0 : 2 * tokens], low)
    slices_ref[:, 0:rows, :] = states.astype(BF16).reshape(chips, rows, width)
    over = jnp.exp(running_t_ref[:, tokens - 1 : tokens])
    over = jnp.broadcast_to(over, (heads, width))
    high = over.astype(BF16).astype(F32)
    middle, low = split(over - high)
    middle, low = middle.astype(F32), low.astype(F32)
    term = iota((8, width), 0)
    for chip in range(chips):
        head = chip * heads // chips
        line = slice(head, head + 1)
        terms = jnp.where(term == 0, high[line], jnp.where(term == 1, middle[line], low[line]))
        slices_ref[chip, rows:, :] = terms.astype(BF16)


def scan_kernel(in_ref, out_ref, before_ref):
    chips, rows, width = out_ref.shape
    first_lanes = iota((rows, width), 1) < width // 2

    def step(k, carried):
        terms = in_ref[k, rows:, :].astype(F32)
        over = terms[0:1, :] + terms[1:2, :] + terms[2:3, :]
        return over * carried + in_ref[k, 0:rows, :].astype(F32)

    def forward(k, carried):
        before_ref[k] = carried
        return step(k, carried)

    def backward(count, carried):
        k = chips - 1 - count
        out_ref[k] = jnp.where(first_lanes, before_ref[k], carried).astype(BF16)
        return step(k, carried)

    start = jnp.zeros((rows, width), F32)
    lax.fori_loop(0, chips, forward, start, unroll=chips <= 16)
    lax.fori_loop(0, chips, backward, start, unroll=chips <= 16)


def inside_kernel(projected_ref, pair_ref, x_hbm, grad_hbm, dt_t_ref, running_t_ref,
                  d_in_hbm, d_proj_ref, scaled_ref, x_ref, grad_ref, d_in_ref,
                  x_sems, grad_sems, out_sems):
    heads, tokens = running_t_ref.shape
    groups = x_sems.shape[0]
    wide = x_ref.shape[1] // groups

    def columns(source, target, sems, group):
        lanes = pl.ds(group * wide, wide)
        return pltpu.make_async_copy(source.at[:, lanes], target.at[:, lanes], sems.at[group])

    x_in = [columns(x_hbm, x_ref, x_sems, group) for group in range(groups)]
    grad_in = [columns(grad_hbm, grad_ref, grad_sems, group) for group in range(groups)]
    d_in_out = [columns(d_in_ref, d_in_hbm, out_sems, group) for group in range(groups)]
    for group in range(groups):
        grad_in[group].start()
        x_in[group].start()
    rows = tokens // 2
    width = projected_ref.shape[1]
    size = grad_ref.shape[1] // heads
    projected = projected_ref[...]
    swapped = pltpu.roll(projected, width // 2, 1)
    first = iota(projected.shape, 1) < width // 2
    scores_t = mm_nt(jnp.where(first, projected, 0.0), swapped, HIGH)
    running_t = running_t_ref[...]
    running = running_t.T
    to_end = (dt_t_ref[...] * jnp.exp(running_t[:, tokens - 1 : tokens] - running_t)).T
    from_start = jnp.exp(running)
    later = iota((rows, rows), 1) >= iota((rows, rows), 0)
    lanes_first = iota((rows, 2 * size), 1) < size
    all_first = iota((tokens, 2 * size), 1) < size
    for pair in range(heads // 2):
        group = 2 * size * pair // wide
        if 2 * size * pair % wide == 0:
            grad_in[group].wait()
            x_in[group].wait()
        lanes = slice(2 * size * pair, 2 * size * (pair + 1))
        even, odd = 2 * pair, 2 * pair + 1
        x_scale = jnp.where(all_first, to_end[:, even : even + 1], to_end[:, odd : odd + 1])
        grad_scale = jnp.where(
            all_first, from_start[:, even : even + 1], from_start[:, odd : odd + 1]
        )
        x_high, x_low = split(x_ref[:, lanes].astype(F32) * x_scale)
        grad_high, grad_low = split(grad_ref[:, lanes].astype(F32) * grad_scale)
        for k, value in enumerate((x_high, grad_high, x_low, grad_low)):
            scaled_ref[k * tokens : (k + 1) * tokens, lanes] = value
        apart = []
        for part in range(2):
            grad = grad_ref[part * rows : (part + 1) * rows, lanes]
            zero = jnp.zeros_like(grad)
            apart.append((jnp.where(lanes_first, grad, zero), jnp.where(lanes_first, zero, grad)))
        for at in range(2):
            here = slice(at * rows, (at + 1) * rows)
            highs, lows, sources = [], [], []
            for to in range(at, 2):
                there = slice(to * rows, (to + 1) * rows)
                for place, head in enumerate((2 * pair, 2 * pair + 1)):
                    spread = running_t[head : head + 1, there] - running[here, head : head + 1]
                    if at == to:
                        spread = jnp.where(later, spread, NEG)
                    high, low = split(jnp.exp(spread) * scores_t[here, there])
                    highs.append(high)
                    lows.append(low)
                    sources.append(apart[to][place])
            sources = jnp.concatenate(sources, axis=0)
            d_in_ref[here, lanes] = mm(jnp.concatenate(highs, axis=1), sources) + mm(
                jnp.concatenate(lows, axis=1), sources
            )
        if 2 * size * (pair + 1) % wide == 0:
            d_in_out[group].start()
    pair_sum = pair_ref[...]
    onto_c = mm(pair_sum, projected, HIGH)
    onto_b = mm(pair_sum.T, projected, HIGH)
    d_proj_ref[...] = pltpu.roll(jnp.where(first, onto_c, onto_b), width // 2, 1)
    for copy in d_in_out:
        copy.wait()


def cross_kernel(arrived_ref, scaled_ref, d_proj_ref, out_ref):
    tokens, width = d_proj_ref.shape
    onto = mm(scaled_ref[...], arrived_ref[...])
    onto = onto[0 : 2 * tokens, :] + onto[2 * tokens :, :]
    first = iota((tokens, width), 1) < width // 2
    crossing = jnp.where(first, onto[tokens:, :], onto[:tokens, :])
    out_ref[...] = d_proj_ref[...] + pltpu.roll(crossing, width // 2, 1)


def term_kernel(mine_ref, other_ref, hidden_t_ref, d_low_ref, term_hbm, term_ref, sem):
    d_low = (mine_ref[...] + other_ref[...]).astype(BF16)
    d_low_ref[...] = d_low
    term_ref[...] = mm(hidden_t_ref[...], d_low)
    store = pltpu.make_async_copy(term_ref, term_hbm, sem.at[0])
    store.start()
    store.wait()


def inputs_kernel(place_ref, arrived_ref, projected_ref, d_in_hbm, dt_t_ref, running_t_ref,
                  d_low_ref, w_ref, mine_ref, send_ref, grad_hidden_ref, d_in_ref, sems):
    heads, tokens = dt_t_ref.shape
    rows = tokens // 2
    width = projected_ref.shape[1]
    size = d_in_ref.shape[1] // heads
    groups = sems.shape[0]
    wide = d_in_ref.shape[1] // groups
    d_in = []
    for group in range(groups):
        lanes = pl.ds(group * wide, wide)
        d_in.append(pltpu.make_async_copy(d_in_hbm.at[:, lanes], d_in_ref.at[:, lanes], sems.at[group]))
        d_in[group].start()
    own = d_low_ref[pl.ds(pl.multiple_of(place_ref[0] * rows, rows), rows), :]
    grad_hidden_ref[...] = mm_nt(own, w_ref[...].reshape(grad_hidden_ref.shape[1], width))
    core = place_ref[0]
    swapped = pltpu.roll(projected_ref[...], width // 2, 1)
    first = iota((tokens, width), 1) < width // 2
    b_high, b_low = split(jnp.where(first, 0.0, swapped))
    b_both = jnp.concatenate([b_high, b_low], axis=0)
    running_t = running_t_ref[...]
    dt = dt_t_ref[...].T
    to_end = jnp.exp(running_t[:, tokens - 1 : tokens] - running_t).T
    lanes_first = iota((tokens, 2 * size), 1) < size
    for pair in range(heads // 2):
        lanes = slice(2 * size * pair, 2 * size * (pair + 1))
        even, odd = 2 * pair, 2 * pair + 1
        if 2 * size * pair % wide == 0:
            d_in[2 * size * pair // wide].wait()
        crossing = mm_nt(b_both, arrived_ref[lanes, :])
        crossing = crossing[:tokens, :] + crossing[tokens:, :]
        decay = jnp.where(lanes_first, to_end[:, even : even + 1], to_end[:, odd : odd + 1])
        step = jnp.where(lanes_first, dt[:, even : even + 1], dt[:, odd : odd + 1])
        grad = step * (d_in_ref[:, lanes] + decay * crossing)
        mine_ref[:, lanes] = jnp.where(core == 0, grad[:rows, :], grad[rows:, :])
        send_ref[:, lanes] = jnp.where(core == 0, grad[rows:, :], grad[:rows, :])


def join_kernel(place_ref, mine_ref, other_ref, out_hbm, sems):
    core = place_ref[0]
    half = mine_ref.shape[1]
    copies = []
    for k, (source, there) in enumerate(((mine_ref, core), (other_ref, 1 - core))):
        lanes = pl.ds(pl.multiple_of(there * half, half), half)
        copies.append(pltpu.make_async_copy(source, out_hbm.at[:, lanes], sems.at[k]))
    for copy in copies:
        copy.start()
    for copy in copies:
        copy.wait()


def sum_kernel(terms_ref, out_ref, *, scale):
    out_ref[...] = jnp.sum(terms_ref[...], axis=0) * scale


def per_device(hidden, x_act, dt_step, log_decay, w_bc, grad_y):
    devices = lax.axis_size("outer") * lax.axis_size("inner")
    rows, model = hidden.shape
    heads = dt_step.shape[1]
    flat = x_act.shape[1]
    w_rows, width = w_bc.shape
    half = flat // 2
    own_heads = heads // 2
    tokens = 2 * rows
    chips = devices // 2
    slice_rows = half // chips
    position = lax.axis_index("outer") * lax.axis_size("inner") + lax.axis_index("inner")
    place = (position & 1).astype(jnp.int32).reshape(1)
    same_core = [list(range(core, devices, 2)) for core in range(2)]

    def exchange(array):
        return lax.all_to_all(
            array, AXES, split_axis=0, concat_axis=0, tiled=True, axis_index_groups=same_core
        )

    def swap(array):
        return lax.ppermute(array, AXES, [(i, i ^ 1) for i in range(devices)])

    spread, small = call(
        spread_kernel,
        (pltpu.HBM((devices, w_rows, width), BF16), shaped((2, heads, rows), F32)), [HBM] * 3,
        [pltpu.VMEM((w_rows, width), BF16), pltpu.VMEM((devices, w_rows, width), BF16),
         pltpu.SemaphoreType.DMA((4,))],
        (HBM, VMEM),
    )(in_hbm(w_bc), in_hbm(dt_step.T), in_hbm(log_decay.T))
    weights = lax.all_to_all(spread, AXES, split_axis=0, concat_axis=0, tiled=True)
    in_kernel = w_rows % 16 == 0
    groups = 4
    hidden_other = swap(hidden)
    hidden_t_rows = model // 2 if in_kernel else 16
    (pair_sum, scaled_t, running_t, dt_t, hidden_both, hidden_t, x_both, grad_both) = call(
        functools.partial(prelude_kernel, parts=w_rows if in_kernel else 0),
        (pltpu.HBM((tokens, tokens), F32), shaped((half, 4 * tokens), BF16),
         shaped((own_heads, tokens), F32), pltpu.HBM((own_heads, tokens), F32),
         shaped((tokens, model), BF16), pltpu.HBM((hidden_t_rows, tokens), BF16),
         pltpu.HBM((tokens, half), BF16), pltpu.HBM((tokens, half), BF16)),
        [SMEM] + [HBM] * 4 + [VMEM] * 2 + [HBM] * 2,
        [pltpu.VMEM((tokens, half), BF16), pltpu.VMEM((tokens, half), BF16),
         pltpu.VMEM((model, tokens), BF16), pltpu.VMEM((hidden_t_rows, tokens), BF16),
         pltpu.VMEM((tokens, tokens), F32), pltpu.VMEM((own_heads, tokens), F32),
         pltpu.SemaphoreType.DMA((2, groups)), pltpu.SemaphoreType.DMA((2, groups)),
         pltpu.SemaphoreType.DMA((2,)), pltpu.SemaphoreType.DMA((5,))],
        (HBM, VMEM, VMEM, HBM, VMEM, HBM, HBM, HBM),
    )(place, in_hbm(x_act), in_hbm(swap(x_act)), in_hbm(grad_y), in_hbm(swap(grad_y)),
      small, swap(small), in_hbm(hidden), hidden_other)
    if not in_kernel:
        weights = weights.reshape(model, width)
        both = jnp.where(place[0] == 0, jnp.concatenate([hidden, hidden_other], axis=0),
                         jnp.concatenate([hidden_other, hidden], axis=0))
        hidden_t = both.T.reshape(chips, 2, w_rows, tokens)
        hidden_t = jnp.where(place[0] == 0, hidden_t[:, 0], hidden_t[:, 1])
        hidden_t = hidden_t.reshape(model // 2, tokens)
    projected, slices = call(
        states_kernel,
        (shaped((tokens, width), F32), shaped((chips, slice_rows + 8, width), BF16)),
        [VMEM] * 4,
    )(hidden_both, weights, scaled_t, running_t)
    slices = exchange(slices)
    d_in, d_inside, scaled = call(
        inside_kernel,
        (pltpu.HBM((tokens, half), F32), shaped((tokens, width), F32),
         shaped((4 * tokens, half), BF16)),
        [VMEM] * 2 + [HBM] * 2 + [VMEM] * 2,
        [pltpu.VMEM((tokens, half), BF16), pltpu.VMEM((tokens, half), BF16),
         pltpu.VMEM((tokens, half), F32)] + [pltpu.SemaphoreType.DMA((groups,))] * 3,
        (HBM, VMEM, VMEM),
    )(projected, pair_sum, in_hbm(x_both), in_hbm(grad_both), dt_t, running_t)
    around = call(
        scan_kernel, shaped((chips, slice_rows, width), BF16), [VMEM],
        [pltpu.VMEM((chips, slice_rows, width), F32)],
    )(slices)
    arrived = exchange(around).reshape(half, width)
    d_part = call(cross_kernel, shaped((tokens, width), F32), [VMEM] * 3)(arrived, scaled, d_inside)
    d_low, term = call(
        term_kernel,
        (shaped((tokens, width), BF16), pltpu.HBM((model // 2, width), F32)), [VMEM] * 3,
        [pltpu.VMEM((model // 2, width), F32), pltpu.SemaphoreType.DMA((1,))], (VMEM, HBM),
    )(d_part, swap(d_part), hidden_t)
    terms = exchange(term.reshape(chips, w_rows, width))
    mine, send, grad_hidden = call(
        inputs_kernel,
        (shaped((rows, half), F32), shaped((rows, half), F32), shaped((rows, model), F32)),
        [SMEM] + [VMEM] * 2 + [HBM] + [VMEM] * 4,
        [pltpu.VMEM((tokens, half), F32), pltpu.SemaphoreType.DMA((groups,))],
    )(place, arrived, projected, in_hbm(d_in), dt_t, running_t, d_low, weights)
    grad_x = call(
        join_kernel, pltpu.HBM((rows, flat), F32), [SMEM] + [VMEM] * 2,
        [pltpu.SemaphoreType.DMA((2,))], HBM,
    )(place, mine, swap(send))
    scale = 1.0 / math.sqrt(rows * devices)
    grad_proj = call(
        functools.partial(sum_kernel, scale=scale), shaped((w_rows, width), F32), [VMEM]
    )(terms)
    return (grad_x, grad_hidden, grad_proj)


def solution(mesh):
    spec = P(AXES, None)

    return jax.shard_map(
        per_device, mesh=mesh, in_specs=(spec,) * 6, out_specs=(spec,) * 3, check_vma=False
    )
```

time: 72.1 us -> 72.9 us (1.011)
  waiting for transfers between devices: 17.2 us -> 9.57 us
  Pallas kernels: 14.7 us -> 18.7 us
  local copies, waits for them, and re-layouts: 0.02 us -> 2.33 us
  blocking collectives: 27 us -> 28.5 us
  starting transfers between devices: 11.2 us -> 12.3 us
  other arithmetic: 0.73 us -> 0 us
    pallas_call x9, Pallas kernels: 9.78 us -> 14.9 us  [the longest x1 4.92 us: per_device(): call(inside_kernel, (pltpu.HBM((tokens, half), F32), shaped((tokens, widt...]
    all_to_all x1, waiting for transfers between devices: 7.95 us -> 3.64 us  [exchange(): lax.all_to_all(array, AXES, split_axis=0, concat_axis=0, tiled=True, axis...]
    all_to_all x1, waiting for transfers between devices: 5.68 us -> 3.3 us  [per_device(): lax.all_to_all(spread, AXES, split_axis=0, concat_axis=0, tiled=True)]
    unnamed x10, local copies, waits for them, and re-layouts: 0.02 us -> 2.33 us
    all_to_all x2, blocking collectives: 27 us -> 28.5 us  [exchange(): lax.all_to_all(array, AXES, split_axis=0, concat_axis=0, tiled=True, axis...]
    ppermute x3 -> x6, starting transfers between devices: 0.33 us -> 1.5 us  [swap(): return lax.ppermute(array, AXES, [(i, i ^ 1) for i in range(devices)])]
    pallas_call x1, Pallas kernels: 4.88 us -> 3.81 us  [per_device(): call(functools.partial(prelude_kernel, parts=w_rows if in_kernel else 0),...]
    ppermute x3 -> x6, waiting for transfers between devices: 3.6 us -> 2.63 us  [swap(): return lax.ppermute(array, AXES, [(i, i ^ 1) for i in range(devices)])]
  transfers between devices with their start and end apart: 5 -> 8, of which waited for: 5 -> 4; matrix products, arithmetic and copies ran while one was open for 0% -> 0% of each run, Pallas kernels for 12% -> 15%
where the time goes in v2:
time: 72.9 us; the launch traced here: 72.1 us
  blocking collectives  28.5 us (39%)
  Pallas kernels  18.7 us (26%)
  starting transfers between devices  12.3 us (17%)
  waiting for transfers between devices  9.57 us (13%)
  local copies, waits for them, and re-layouts  2.33 us (3%)
  between operations  0.75 us (1%)
    all_to_all x2, blocking collectives, exchange(): lax.all_to_all(array, AXES, split_axis=0, concat_axis=0, tiled=True, axis...  28.5 us
    all_to_all x1, starting transfers between devices, per_device(): lax.all_to_all(spread, AXES, split_axis=0, concat_axis=0, tiled=True)  7.27 us
    pallas_call x1, Pallas kernels, per_device(): call(inside_kernel, (pltpu.HBM((tokens, half), F32), shaped((tokens, widt...  4.92 us
    pallas_call x1, Pallas kernels, per_device(): call(functools.partial(prelude_kernel, parts=w_rows if in_kernel else 0),...  3.81 us
    all_to_all x1, waiting for transfers between devices, exchange(): lax.all_to_all(array, AXES, split_axis=0, concat_axis=0, tiled=True, axis...  3.64 us
    all_to_all x1, starting transfers between devices, exchange(): lax.all_to_all(array, AXES, split_axis=0, concat_axis=0, tiled=True, axis...  3.53 us
    all_to_all x1, waiting for transfers between devices, per_device(): lax.all_to_all(spread, AXES, split_axis=0, concat_axis=0, tiled=True)  3.3 us
    pallas_call x1, Pallas kernels, per_device(): call(inputs_kernel, (shaped((rows, half), F32), shaped((rows, half), F32)...  3.06 us
  transfers between devices with their start and end apart: 8, of which 4 were waited for; matrix products, arithmetic and copies ran while one was open for 0% of the time, Pallas kernels for 15%

profile of v2, /device:TPU:0, one launch (start us, length us, event | category | flops | bytes accessed | tf_op | source)
XLA Modules:
  0.0 72.1 jit_solution(9623140751234574569)
XLA Ops:
  0.6 0.6 collective-permute-start
  1.2 0.1 collective-permute-start.1
  1.3 1.5 %shard_map.85 = (bf16[32,32,128]{2,1,0:T(8,128)(2,1)}, f32[2,32,128]{2,1,0:T(8,128)S(1)}) custom-call(bf16[32,128]{1,0:T(8,128)(2,1)} %w_hbm.1, f32[32,128]{1,0:T(8,128)} %bitcast.8, f32[32,128]{1,0:T(8,128)} %bitcast.9), custom_call_target="tpu_custom_call" | custom-call | tf_op jit(solution)/shard_map/pallas_call | solution.py:420
  2.8 7.3 %all-to-all-start = ((bf16[32,32,128]{2,1,0:T(8,128)(2,1)}), bf16[32,32,128]{2,1,0:T(8,128)(2,1)S(1)}, u32[]{:S(2)}, u32[]{:S(2)}) async-start(bf16[32,32,128]{2,1,0:T(8,128)(2,1)} %get-tuple-element.25), calls=%async_computation | async-start | bytes 524288 | tf_op jit(solution)/shard_map/all_to_all | solution.py:427
  10.0 0.3 collective-permute-start.3
  10.4 0.3 collective-permute-start.2
  10.6 1.3 %collective-permute-done.2.small_other_ref = f32[2,32,128]{2,1,0:T(8,128)S(1)} collective-permute-done((f32[2,32,128]{2,1,0:T(8,128)S(1)}, f32[2,32,128]{2,1,0:T(8,128)S(1)}, u32[]{:S(2)}, u32[]{:S(2)}) %collective-permute-start.2) | collective-permute-done | bytes 32800 | tf_op jit(solution)/shard_map/ppermute | solution.py:418
  11.9 0.0 collective-permute-done.3.hidden_other_hbm
  11.9 0.0 collective-permute-done.x_other_hbm
  11.9 0.0 copy-start.3
  11.9 0.0 collective-permute-done.1.grad_other_hbm
  11.9 0.8 %copy-done.3 = bf16[128,2048]{1,0:T(8,128)(2,1)} copy-done((bf16[128,2048]{1,0:T(8,128)(2,1)}, bf16[128,2048]{1,0:T(8,128)(2,1)S(1)}, u32[]{:S(2)}) %copy-start.3) | copy-done | bytes 524312
  12.7 0.0 copy-start.4
  12.7 0.8 %copy-done.4 = bf16[128,2048]{1,0:T(8,128)(2,1)} copy-done((bf16[128,2048]{1,0:T(8,128)(2,1)}, bf16[128,2048]{1,0:T(8,128)(2,1)S(1)}, u32[]{:S(2)}) %copy-start.4) | copy-done | bytes 524312
  13.5 3.8 %shard_map.86 = (f32[256,256]{1,0:T(8,128)}, bf16[1024,1024]{1,0:T(8,128)(2,1)S(1)}, f32[16,256]{1,0:T(8,128)S(1)}, f32[16,256]{1,0:T(8,128)}, bf16[256,1024]{1,...) custom-call(s32[1]{0:T(128)} %bitcast.place_ref, ...), custom_call_target="tpu_custom_call" | custom-call | tf_op jit(solution)/shard_map/pallas_call | solution.py:432
  17.3 3.3 %all-to-all-done.w_ref = bf16[32,32,128]{2,1,0:T(8,128)(2,1)S(1)} async-done(((bf16[32,32,128]{2,1,0:T(8,128)(2,1)}), bf16[32,32,128]{2,1,0:T(8,128)(2,1)S(1)}, u32[]{:S(2)}, u32[]{:S(2)}) %all-to-all-start) | async-done | bytes 262176 | tf_op jit(solution)/shard_map/all_to_all | solution.py:427
  20.6 0.0 copy-start.1
  20.6 1.2 %shard_map.87 = (f32[256,128]{1,0:T(8,128)S(1)}, bf16[16,72,128]{2,1,0:T(8,128)(2,1)S(1)}) custom-call(bf16[256,1024]{1,0:T(8,128)(2,1)S(1)} %get-tuple-element.24.hidden_ref, bf16[32,32,128]{2,1,0:T(8,128)(2,1)S(1)} %all-to-all-done.w_ref, bf16[1024,1024]{1,0:T(8,128)(2,1)S(1)} %get-tuple-element.26.scaled_t_ref, f32[16,256]{1,0:T(8,128)S(1)} %get-tuple-element.27.running_t_ref), custom_call_target="tpu_custom_call" | custom-call | tf_op jit(solution)/shard_map/pallas_call | solution.py:454
  21.8 14.3 %all_to_all.20.in_ref = bf16[16,72,128]{2,1,0:T(8,128)(2,1)S(1)} all-to-all(bf16[16,72,128]{2,1,0:T(8,128)(2,1)S(1)} %get-tuple-element.28), channel_id=1, replica_groups={{0,2,4,6,8,10,12,14,16,18,20,22,24,26,28,30},{1,3,5,7,9,11,13,15,17,19,..., dimensions={0} | all-to-all | bytes 589824 | tf_op jit(solution)/shard_map/all_to_all | solution.py:413
  36.2 0.9 %shard_map.88 = bf16[16,64,128]{2,1,0:T(8,128)(2,1)} custom-call(bf16[16,72,128]{2,1,0:T(8,128)(2,1)S(1)} %all_to_all.20.in_ref), custom_call_target="tpu_custom_call" | custom-call | tf_op jit(solution)/shard_map/pallas_call | solution.py:469
  37.0 3.5 %all-to-all-start.2 = ((bf16[16,64,128]{2,1,0:T(8,128)(2,1)}), bf16[16,64,128]{2,1,0:T(8,128)(2,1)S(1)}, u32[]{:S(2)}, u32[]{:S(2)}) async-start(bf16[16,64,128]{2,1,0:T(8,128)(2,1)} %shard_map.88), calls=%async_computation.2 | async-start | bytes 524288 | tf_op jit(solution)/shard_map/all_to_all | solution.py:413
  40.6 0.0 copy-start
  40.6 0.0 copy-done.1
  40.6 0.0 copy-start.2
  40.6 0.7 %copy-done.2 = f32[16,256]{1,0:T(8,128)S(1)} copy-done((f32[16,256]{1,0:T(8,128)S(1)}, f32[16,256]{1,0:T(8,128)}, u32[]{:S(2)}) %copy-start.2) | copy-done | bytes 16408
  41.4 4.9 %shard_map.89 = (f32[256,1024]{1,0:T(8,128)}, f32[256,128]{1,0:T(8,128)S(1)}, bf16[1024,1024]{1,0:T(8,128)(2,1)S(1)}) custom-call(f32[256,128]{1,0:T(8,128)S(1)} %get-tuple-element.29.projected_ref, f32[256,256]{1,0:T(8,128)S(1)} %copy-done.1, bf16[256,1024]{1,0:T(8,128)(2,1)} %get-tuple-element.31.x_hbm, bf16[256,1024]{1,0:T(8,128)(2,1)} %get-tuple-element.32.grad_hbm, ...), custom_call_target="tpu_custom_call" | custom-call | tf_op jit(solution)/shard_map/pallas_call | solution.py:460
  46.3 3.6 %all-to-all-done.2 = bf16[16,64,128]{2,1,0:T(8,128)(2,1)S(1)} async-done(((bf16[16,64,128]{2,1,0:T(8,128)(2,1)}), bf16[16,64,128]{2,1,0:T(8,128)(2,1)S(1)}, u32[]{:S(2)}, u32[]{:S(2)}) %all-to-all-start.2) | async-done | bytes 262176 | tf_op jit(solution)/shard_map/all_to_all | solution.py:413
  49.9 0.8 %shard_map.90.mine_ref = f32[256,128]{1,0:T(8,128)S(1)} custom-call(bf16[1024,128]{1,0:T(8,128)(2,1)S(1)} %bitcast.5, bf16[1024,1024]{1,0:T(8,128)(2,1)S(1)} %get-tuple-element.35.scaled_ref, f32[256,128]{1,0:T(8,128)S(1)} %get-tuple-element.36.d_proj_ref), custom_call_target="tpu_custom_call" | custom-call | tf_op jit(solution)/shard_map/pallas_call | solution.py:474
  50.7 0.1 collective-permute-start.4
  50.8 1.3 %collective-permute-done.4.other_ref = f32[256,128]{1,0:T(8,128)S(1)} collective-permute-done((f32[256,128]{1,0:T(8,128)S(1)}, f32[256,128]{1,0:T(8,128)S(1)}, u32[]{:S(2)}, u32[]{:S(2)}) %collective-permute-start.4) | collective-permute-done | bytes 131104 | tf_op jit(solution)/shard_map/ppermute | solution.py:418
  52.1 0.0 copy-done
  52.1 0.9 %shard_map.91 = (bf16[256,128]{1,0:T(8,128)(2,1)S(1)}, f32[512,128]{1,0:T(8,128)}) custom-call(f32[256,128]{1,0:T(8,128)S(1)} %shard_map.90.mine_ref, f32[256,128]{1,0:T(8,128)S(1)} %collective-permute-done.4.other_ref, bf16[512,256]{1,0:T(8,128)(2,1)S(1)} %copy-done), custom_call_target="tpu_custom_call" | custom-call | tf_op jit(solution)/shard_map/pallas_call | solution.py:475
  53.1 3.1 %shard_map.92 = (f32[128,1024]{1,0:T(8,128)S(1)}, f32[128,1024]{1,0:T(8,128)S(1)}, f32[128,1024]{1,0:T(8,128)}) custom-call(s32[1]{0:T(128)} %bitcast.place_ref, bf16[1024,128]{1,0:T(8,128)(2,1)S(1)} %bitcast.6, f32[256,128]{1,0:T(8,128)S(1)} %get-tuple-element.29.projected_ref, f32[256,1024]{1,0:T(8,128)} %get-tuple-element.34.d_in_hbm, ...), custom_call_target="tpu_custom_call" | custom-call | tf_op jit(solution)/shard_map/pallas_call | solution.py:481
  56.2 0.2 collective-permute-start.5
  56.4 14.1 %all_to_all.21.terms_ref = f32[16,32,128]{2,1,0:T(8,128)S(1)} all-to-all(f32[16,32,128]{2,1,0:T(8,128)} %bitcast.7), channel_id=1, replica_groups={{0,2,4,6,8,10,12,14,16,18,20,22,24,26,28,30},{1,3,5,7,9,11,13,15,17,19,..., dimensions={0} | all-to-all | bytes 524288 | tf_op jit(solution)/shard_map/all_to_all | solution.py:413
  70.5 0.6 shard_map.94
  71.1 0.0 collective-permute-done.5.other_ref
  71.1 1.0 %shard_map.93 = f32[128,2048]{1,0:T(8,128)} custom-call(s32[1]{0:T(128)} %bitcast.place_ref, f32[128,1024]{1,0:T(8,128)S(1)} %get-tuple-element.39.mine_ref, f32[128,1024]{1,0:T(8,128)S(1)} %collective-permute-done.5.other_ref), custom_call_target="tpu_custom_call" | custom-call | tf_op jit(solution)/shard_map/pallas_call | solution.py:487
Async XLA Ops:
  0.6 11.3 %collective-permute-start = (bf16[128,2048]{1,0:T(8,128)(2,1)}, bf16[128,2048]{1,0:T(8,128)(2,1)S(1)}, u32[]{:S(2)}, u32[]{:S(2)}) collective-permute-start(bf16[128,2048]{1,0:T(8,128)(2,1)} %x_hbm.1), channel_id=1, source_target_pairs={{0,1},{1,0},{2,3},{3,2},{4,5},{5,4},{6,7},{7,6},{8,9},{9,8},{10,11... | collective-permute-start | bytes 1572872 | tf_op jit(solution)/shard_map/ppermute | solution.py:418
  1.2 10.7 %collective-permute-start.1 = (bf16[128,2048]{1,0:T(8,128)(2,1)}, bf16[128,2048]{1,0:T(8,128)(2,1)S(1)}, u32[]{:S(2)}, u32[]{:S(2)}) collective-permute-start(bf16[128,2048]{1,0:T(8,128)(2,1)} %grad_hbm.1), channel_id=1, source_target_pairs={{0,1},{1,0},{2,3},{3,2},{4,5},{5,4},{6,7},{7,6},{8,9},{9,8},{10,11... | collective-permute-start | bytes 1572872 | tf_op jit(solution)/shard_map/ppermute | solution.py:418
  2.8 17.8 %all-to-all-start = ((bf16[32,32,128]{2,1,0:T(8,128)(2,1)}), bf16[32,32,128]{2,1,0:T(8,128)(2,1)S(1)}, u32[]{:S(2)}, u32[]{:S(2)}) async-start(bf16[32,32,128]{2,1,0:T(8,128)(2,1)} %get-tuple-element.25), calls=%async_computation | async-start | bytes 524288 | tf_op jit(solution)/shard_map/all_to_all | solution.py:427
  10.0 1.9 %collective-permute-start.3 = (bf16[128,1024]{1,0:T(8,128)(2,1)}, bf16[128,1024]{1,0:T(8,128)(2,1)S(1)}, u32[]{:S(2)}, u32[]{:S(2)}) collective-permute-start(bf16[128,1024]{1,0:T(8,128)(2,1)} %hidden_hbm.1), channel_id=1, source_target_pairs={{0,1},{1,0},{2,3},{3,2},{4,5},{5,4},{6,7},{7,6},{8,9},{9,8},{10,11... | collective-permute-start | bytes 786440 | tf_op jit(solution)/shard_map/ppermute | solution.py:418
  10.4 1.5 %collective-permute-start.2 = (f32[2,32,128]{2,1,0:T(8,128)S(1)}, f32[2,32,128]{2,1,0:T(8,128)S(1)}, u32[]{:S(2)}, u32[]{:S(2)}) collective-permute-start(f32[2,32,128]{2,1,0:T(8,128)S(1)} %get-tuple-element.23.small_ref), channel_id=1, source_target_pairs={{0,1},{1,0},{2,3},{3,2},{4,5},{5,4},{6,7},{7,6},{8,9},{9,8},{10,11... | collective-permute-start | bytes 98312 | tf_op jit(solution)/shard_map/ppermute | solution.py:418
  11.9 0.8 %copy-start.3 = (bf16[128,2048]{1,0:T(8,128)(2,1)}, bf16[128,2048]{1,0:T(8,128)(2,1)S(1)}, u32[]{:S(2)}) copy-start(bf16[128,2048]{1,0:T(8,128)(2,1)S(1)} %collective-permute-done.x_other_hbm) | copy-start | bytes 1572868
  12.7 0.8 %copy-start.4 = (bf16[128,2048]{1,0:T(8,128)(2,1)}, bf16[128,2048]{1,0:T(8,128)(2,1)S(1)}, u32[]{:S(2)}) copy-start(bf16[128,2048]{1,0:T(8,128)(2,1)S(1)} %collective-permute-done.1.grad_other_hbm) | copy-start | bytes 1572868
  20.6 20.0 %copy-start.1 = (f32[256,256]{1,0:T(8,128)S(1)}, f32[256,256]{1,0:T(8,128)}, u32[]{:S(2)}) copy-start(f32[256,256]{1,0:T(8,128)} %get-tuple-element.30.pair_ref) | copy-start | bytes 786436
  37.0 12.9 %all-to-all-start.2 = ((bf16[16,64,128]{2,1,0:T(8,128)(2,1)}), bf16[16,64,128]{2,1,0:T(8,128)(2,1)S(1)}, u32[]{:S(2)}, u32[]{:S(2)}) async-start(bf16[16,64,128]{2,1,0:T(8,128)(2,1)} %shard_map.88), calls=%async_computation.2 | async-start | bytes 524288 | tf_op jit(solution)/shard_map/all_to_all | solution.py:413
  40.6 11.5 %copy-start = (bf16[512,256]{1,0:T(8,128)(2,1)S(1)}, bf16[512,256]{1,0:T(8,128)(2,1)}, u32[]{:S(2)}) copy-start(bf16[512,256]{1,0:T(8,128)(2,1)} %get-tuple-element.37.hidden_t_ref) | copy-start | bytes 786436
  40.6 0.8 %copy-start.2 = (f32[16,256]{1,0:T(8,128)S(1)}, f32[16,256]{1,0:T(8,128)}, u32[]{:S(2)}) copy-start(f32[16,256]{1,0:T(8,128)} %get-tuple-element.33.dt_t_ref) | copy-start | bytes 49156
  50.7 1.4 %collective-permute-start.4 = (f32[256,128]{1,0:T(8,128)S(1)}, f32[256,128]{1,0:T(8,128)S(1)}, u32[]{:S(2)}, u32[]{:S(2)}) collective-permute-start(f32[256,128]{1,0:T(8,128)S(1)} %shard_map.90.mine_ref), channel_id=1, source_target_pairs={{0,1},{1,0},{2,3},{3,2},{4,5},{5,4},{6,7},{7,6},{8,9},{9,8},{10,11... | collective-permute-start | bytes 393224 | tf_op jit(solution)/shard_map/ppermute | solution.py:418
  56.2 15.0 %collective-permute-start.5 = (f32[128,1024]{1,0:T(8,128)S(1)}, f32[128,1024]{1,0:T(8,128)S(1)}, u32[]{:S(2)}, u32[]{:S(2)}) collective-permute-start(f32[128,1024]{1,0:T(8,128)S(1)} %get-tuple-element.40), channel_id=1, source_target_pairs={{0,1},{1,0},{2,3},{3,2},{4,5},{5,4},{6,7},{7,6},{8,9},{9,8},{10,11... | collective-permute-start | bytes 1572872 | tf_op jit(solution)/shard_map/ppermute | solution.py:418

commit v3 on v2

--- a/solution.py
+++ b/solution.py
@@ -220,7 +220,7 @@
         slices_ref[chip, rows:, :] = terms.astype(BF16)
 
 
-def scan_kernel(in_ref, out_ref, before_ref):
+def scan_kernel(in_ref, out_hbm, before_ref, out_ref, sems):
     chips, rows, width = out_ref.shape
     first_lanes = iota((rows, width), 1) < width // 2
 
@@ -236,11 +236,20 @@
     def backward(count, carried):
         k = chips - 1 - count
         out_ref[k] = jnp.where(first_lanes, before_ref[k], carried).astype(BF16)
+        store(k).start()
         return step(k, carried)
+
+    def store(k):
+        return pltpu.make_async_copy(out_ref.at[k], out_hbm.at[k], sems.at[k])
+
+    def finish(k, _):
+        store(k).wait()
+        return 0
 
     start = jnp.zeros((rows, width), F32)
     lax.fori_loop(0, chips, forward, start, unroll=chips <= 16)
     lax.fori_loop(0, chips, backward, start, unroll=chips <= 16)
+    lax.fori_loop(0, chips, finish, 0, unroll=chips <= 16)
 
 
 def inside_kernel(projected_ref, pair_ref, x_hbm, grad_hbm, dt_t_ref, running_t_ref,
@@ -330,51 +339,72 @@
     out_ref[...] = d_proj_ref[...] + pltpu.roll(crossing, width // 2, 1)
 
 
-def term_kernel(mine_ref, other_ref, hidden_t_ref, d_low_ref, term_hbm, term_ref, sem):
+def term_kernel(mine_ref, other_ref, hidden_t_ref, d_low_ref, term_hbm, term_ref, sems):
+    chips, chunk, _ = term_ref.shape
+    rows = hidden_t_ref.shape[0] // chips
     d_low = (mine_ref[...] + other_ref[...]).astype(BF16)
     d_low_ref[...] = d_low
-    term_ref[...] = mm(hidden_t_ref[...], d_low)
-    store = pltpu.make_async_copy(term_ref, term_hbm, sem.at[0])
-    store.start()
-    store.wait()
-
-
-def inputs_kernel(place_ref, arrived_ref, projected_ref, d_in_hbm, dt_t_ref, running_t_ref,
-                  d_low_ref, w_ref, mine_ref, send_ref, grad_hidden_ref, d_in_ref, sems):
+    parts = sems.shape[0]
+    stores = []
+    for part in range(parts):
+        first, count = part * chips // parts, chips // parts
+        term = mm(hidden_t_ref[first * rows : (first + count) * rows, :], d_low)
+        for k in range(count):
+            block = term[k * rows : (k + 1) * rows, :]
+            high = block.astype(BF16).astype(F32)
+            rest = (block - high)[0 : chunk - rows, :]
+            term_ref[first + k] = jnp.concatenate([high, rest], axis=0).astype(BF16)
+        there = pl.ds(first, count)
+        stores.append(pltpu.make_async_copy(term_ref.at[there], term_hbm.at[there], sems.at[part]))
+        stores[-1].start()
+    for store in stores:
+        store.wait()
+
+
+def inputs_kernel(place_ref, arrived_ref, projected_ref, d_in_hbm, dt_t_ref, running_t_ref, *rest, other):
+    if other:
+        grad_ref, d_in_ref, sems = rest
+    else:
+        d_low_ref, w_ref, grad_ref, grad_hidden_ref, d_in_ref, sems = rest
     heads, tokens = dt_t_ref.shape
     rows = tokens // 2
     width = projected_ref.shape[1]
     size = d_in_ref.shape[1] // heads
+    which = 1 - place_ref[0] if other else place_ref[0]
+    here = pl.ds(pl.multiple_of(which * rows, rows), rows)
     groups = sems.shape[0]
     wide = d_in_ref.shape[1] // groups
     d_in = []
     for group in range(groups):
         lanes = pl.ds(group * wide, wide)
-        d_in.append(pltpu.make_async_copy(d_in_hbm.at[:, lanes], d_in_ref.at[:, lanes], sems.at[group]))
+        d_in.append(pltpu.make_async_copy(d_in_hbm.at[here, lanes], d_in_ref.at[:, lanes], sems.at[group]))
         d_in[group].start()
-    own = d_low_ref[pl.ds(pl.multiple_of(place_ref[0] * rows, rows), rows), :]
-    grad_hidden_ref[...] = mm_nt(own, w_ref[...].reshape(grad_hidden_ref.shape[1], width))
-    core = place_ref[0]
-    swapped = pltpu.roll(projected_ref[...], width // 2, 1)
-    first = iota((tokens, width), 1) < width // 2
+    if not other:
+        grad_hidden_ref[...] = mm_nt(
+            d_low_ref[here, :], w_ref[...].reshape(grad_hidden_ref.shape[1], width)
+        )
+    swapped = pltpu.roll(projected_ref[here, :], width // 2, 1)
+    first = iota((rows, width), 1) < width // 2
     b_high, b_low = split(jnp.where(first, 0.0, swapped))
     b_both = jnp.concatenate([b_high, b_low], axis=0)
     running_t = running_t_ref[...]
-    dt = dt_t_ref[...].T
-    to_end = jnp.exp(running_t[:, tokens - 1 : tokens] - running_t).T
-    lanes_first = iota((tokens, 2 * size), 1) < size
+    to_end_t = jnp.exp(running_t[:, tokens - 1 : tokens] - running_t)
+
+    def columns(both):
+        return jnp.where(which == 0, both[:, :rows], both[:, rows:]).T
+
+    dt, to_end = columns(dt_t_ref[...]), columns(to_end_t)
+    lanes_first = iota((rows, 2 * size), 1) < size
     for pair in range(heads // 2):
         lanes = slice(2 * size * pair, 2 * size * (pair + 1))
         even, odd = 2 * pair, 2 * pair + 1
         if 2 * size * pair % wide == 0:
             d_in[2 * size * pair // wide].wait()
         crossing = mm_nt(b_both, arrived_ref[lanes, :])
-        crossing = crossing[:tokens, :] + crossing[tokens:, :]
+        crossing = crossing[:rows, :] + crossing[rows:, :]
         decay = jnp.where(lanes_first, to_end[:, even : even + 1], to_end[:, odd : odd + 1])
         step = jnp.where(lanes_first, dt[:, even : even + 1], dt[:, odd : odd + 1])
-        grad = step * (d_in_ref[:, lanes] + decay * crossing)
-        mine_ref[:, lanes] = jnp.where(core == 0, grad[:rows, :], grad[rows:, :])
-        send_ref[:, lanes] = jnp.where(core == 0, grad[rows:, :], grad[:rows, :])
+        grad_ref[:, lanes] = step * (d_in_ref[:, lanes] + decay * crossing)
 
 
 def join_kernel(place_ref, mine_ref, other_ref, out_hbm, sems):
@@ -391,7 +421,11 @@
 
 
 def sum_kernel(terms_ref, out_ref, *, scale):
-    out_ref[...] = jnp.sum(terms_ref[...], axis=0) * scale
+    rows = out_ref.shape[0]
+    more = terms_ref.shape[1] - rows
+    terms = jnp.sum(terms_ref[...].astype(F32), axis=0)
+    out_ref[0:more, :] = (terms[0:more, :] + terms[rows:, :]) * scale
+    out_ref[more:, :] = terms[more:rows, :] * scale
 
 
 def per_device(hidden, x_act, dt_step, log_decay, w_bc, grad_y):
@@ -467,27 +501,36 @@
         (HBM, VMEM, VMEM),
     )(projected, pair_sum, in_hbm(x_both), in_hbm(grad_both), dt_t, running_t)
     around = call(
-        scan_kernel, shaped((chips, slice_rows, width), BF16), [VMEM],
-        [pltpu.VMEM((chips, slice_rows, width), F32)],
+        scan_kernel, pltpu.HBM((chips, slice_rows, width), BF16), [VMEM],
+        [pltpu.VMEM((chips, slice_rows, width), F32), pltpu.VMEM((chips, slice_rows, width), BF16),
+         pltpu.SemaphoreType.DMA((chips,))],
+        HBM,
     )(slices)
     arrived = exchange(around).reshape(half, width)
     d_part = call(cross_kernel, shaped((tokens, width), F32), [VMEM] * 3)(arrived, scaled, d_inside)
+    term_rows = w_rows + w_rows // 2
     d_low, term = call(
         term_kernel,
-        (shaped((tokens, width), BF16), pltpu.HBM((model // 2, width), F32)), [VMEM] * 3,
-        [pltpu.VMEM((model // 2, width), F32), pltpu.SemaphoreType.DMA((1,))], (VMEM, HBM),
+        (shaped((tokens, width), BF16), pltpu.HBM((chips, term_rows, width), BF16)), [VMEM] * 3,
+        [pltpu.VMEM((chips, term_rows, width), BF16), pltpu.SemaphoreType.DMA((4,))], (VMEM, HBM),
     )(d_part, swap(d_part), hidden_t)
-    terms = exchange(term.reshape(chips, w_rows, width))
-    mine, send, grad_hidden = call(
-        inputs_kernel,
-        (shaped((rows, half), F32), shaped((rows, half), F32), shaped((rows, model), F32)),
-        [SMEM] + [VMEM] * 2 + [HBM] + [VMEM] * 4,
-        [pltpu.VMEM((tokens, half), F32), pltpu.SemaphoreType.DMA((groups,))],
-    )(place, arrived, projected, in_hbm(d_in), dt_t, running_t, d_low, weights)
+    terms = exchange(term)
+    d_in = in_hbm(d_in)
+    in_specs = [SMEM] + [VMEM] * 2 + [HBM] + [VMEM] * 2
+    scratch = [pltpu.VMEM((rows, half), F32), pltpu.SemaphoreType.DMA((groups,))]
+    send = call(
+        functools.partial(inputs_kernel, other=True), shaped((rows, half), F32), in_specs,
+        scratch,
+    )(place, arrived, projected, d_in, dt_t, running_t)
+    come = swap(send)
+    mine, grad_hidden = call(
+        functools.partial(inputs_kernel, other=False),
+        (shaped((rows, half), F32), shaped((rows, model), F32)), in_specs + [VMEM] * 2, scratch,
+    )(place, arrived, projected, d_in, dt_t, running_t, d_low, weights)
     grad_x = call(
         join_kernel, pltpu.HBM((rows, flat), F32), [SMEM] + [VMEM] * 2,
         [pltpu.SemaphoreType.DMA((2,))], HBM,
-    )(place, mine, swap(send))
+    )(place, mine, come)
     scale = 1.0 / math.sqrt(rows * devices)
     grad_proj = call(
         functools.partial(sum_kernel, scale=scale), shaped((w_rows, width), F32), [VMEM]

time: 72.9 us -> 71.6 us (0.982)
  blocking collectives: 28.5 us -> 14.4 us
  waiting for transfers between devices: 9.57 us -> 15.3 us
  starting transfers between devices: 12.3 us -> 16.5 us
  Pallas kernels: 18.7 us -> 20.9 us
    all_to_all x2 -> x1, blocking collectives: 28.5 us -> 14.4 us  [exchange(): lax.all_to_all(array, AXES, split_axis=0, concat_axis=0, tiled=True, axis...]
    all_to_all x1 -> x2, waiting for transfers between devices: 3.64 us -> 9.68 us  [exchange(): lax.all_to_all(array, AXES, split_axis=0, concat_axis=0, tiled=True, axis...]
    all_to_all x1 -> x2, starting transfers between devices: 3.53 us -> 7.41 us  [exchange(): lax.all_to_all(array, AXES, split_axis=0, concat_axis=0, tiled=True, axis...]
    pallas_call x3 -> x4, Pallas kernels: 4.86 us -> 7.08 us  [the longest x1 2.72 us: per_device(): call(functools.partial(inputs_kernel, other=True), shaped((rows, half), F...]
    unnamed x10 -> x18, local copies, waits for them, and re-layouts: 2.33 us -> 2.97 us
  transfers between devices with their start and end apart: 8 -> 9, of which waited for: 4 -> 5; matrix products, arithmetic and copies ran while one was open for 0% -> 0% of each run, Pallas kernels for 15% -> 21%
where the time goes in v3:
time: 71.6 us; the launch traced here: 70.8 us
  Pallas kernels  20.9 us (29%)
  starting transfers between devices  16.5 us (23%)
  waiting for transfers between devices  15.3 us (21%)
  blocking collectives  14.4 us (20%)
  local copies, waits for them, and re-layouts  2.97 us (4%)
  between operations  0.8 us (1%)
    all_to_all x1, blocking collectives, exchange(): lax.all_to_all(array, AXES, split_axis=0, concat_axis=0, tiled=True, axis...  14.4 us
    all_to_all x2, waiting for transfers between devices, exchange(): lax.all_to_all(array, AXES, split_axis=0, concat_axis=0, tiled=True, axis...  9.68 us
    all_to_all x2, starting transfers between devices, exchange(): lax.all_to_all(array, AXES, split_axis=0, concat_axis=0, tiled=True, axis...  7.41 us
    all_to_all x1, starting transfers between devices, per_device(): lax.all_to_all(spread, AXES, split_axis=0, concat_axis=0, tiled=True)  7.27 us
    pallas_call x1, Pallas kernels, per_device(): call(inside_kernel, (pltpu.HBM((tokens, half), F32), shaped((tokens, widt...  4.92 us
    pallas_call x1, Pallas kernels, per_device(): call(functools.partial(prelude_kernel, parts=w_rows if in_kernel else 0),...  3.81 us
    all_to_all x1, waiting for transfers between devices, per_device(): lax.all_to_all(spread, AXES, split_axis=0, concat_axis=0, tiled=True)  3.3 us
    unnamed x18, local copies, waits for them, and re-layouts  2.97 us
  transfers between devices with their start and end apart: 9, of which 5 were waited for; matrix products, arithmetic and copies ran while one was open for 0% of the time, Pallas kernels for 21%

profile of v3, /device:TPU:0, one launch (start us, length us, event | category | flops | bytes accessed | tf_op | source)
XLA Modules:
  0.0 70.8 jit_solution(8301777310510870531)
XLA Ops:
  0.6 0.6 collective-permute-start
  1.2 0.1 collective-permute-start.1
  1.3 1.5 %shard_map.85 = (bf16[32,32,128]{2,1,0:T(8,128)(2,1)}, f32[2,32,128]{2,1,0:T(8,128)S(1)}) custom-call(bf16[32,128]{1,0:T(8,128)(2,1)} %w_hbm.1, f32[32,128]{1,0:T(8,128)} %bitcast.7, f32[32,128]{1,0:T(8,128)} %bitcast.8), custom_call_target="tpu_custom_call" | custom-call | tf_op jit(solution)/shard_map/pallas_call | solution.py:454
  2.7 7.3 %all-to-all-start = ((bf16[32,32,128]{2,1,0:T(8,128)(2,1)}), bf16[32,32,128]{2,1,0:T(8,128)(2,1)S(1)}, u32[]{:S(2)}, u32[]{:S(2)}) async-start(bf16[32,32,128]{2,1,0:T(8,128)(2,1)} %get-tuple-element.24), calls=%async_computation | async-start | bytes 524288 | tf_op jit(solution)/shard_map/all_to_all | solution.py:461
  10.0 0.3 collective-permute-start.3
  10.3 0.3 collective-permute-start.2
  10.6 1.3 %collective-permute-done.2.small_other_ref = f32[2,32,128]{2,1,0:T(8,128)S(1)} collective-permute-done((f32[2,32,128]{2,1,0:T(8,128)S(1)}, f32[2,32,128]{2,1,0:T(8,128)S(1)}, u32[]{:S(2)}, u32[]{:S(2)}) %collective-permute-start.2) | collective-permute-done | bytes 32800 | tf_op jit(solution)/shard_map/ppermute | solution.py:452
  11.9 0.0 collective-permute-done.3.hidden_other_hbm
  11.9 0.0 collective-permute-done.x_other_hbm
  11.9 0.0 copy-start.7
  11.9 0.0 collective-permute-done.1.grad_other_hbm
  11.9 0.8 %copy-done.7 = bf16[128,2048]{1,0:T(8,128)(2,1)} copy-done((bf16[128,2048]{1,0:T(8,128)(2,1)}, bf16[128,2048]{1,0:T(8,128)(2,1)S(1)}, u32[]{:S(2)}) %copy-start.7) | copy-done | bytes 524312
  12.7 0.0 copy-start.8
  12.7 0.8 %copy-done.8 = bf16[128,2048]{1,0:T(8,128)(2,1)} copy-done((bf16[128,2048]{1,0:T(8,128)(2,1)}, bf16[128,2048]{1,0:T(8,128)(2,1)S(1)}, u32[]{:S(2)}) %copy-start.8) | copy-done | bytes 524312
  13.5 3.8 %shard_map.86 = (f32[256,256]{1,0:T(8,128)}, bf16[1024,1024]{1,0:T(8,128)(2,1)S(1)}, f32[16,256]{1,0:T(8,128)S(1)}, f32[16,256]{1,0:T(8,128)}, bf16[256,1024]{1,...) custom-call(s32[1]{0:T(128)} %bitcast.place_ref, ...), custom_call_target="tpu_custom_call" | custom-call | tf_op jit(solution)/shard_map/pallas_call | solution.py:466
  17.3 3.3 %all-to-all-done.w_ref.rest_1_ = bf16[32,32,128]{2,1,0:T(8,128)(2,1)S(1)} async-done(((bf16[32,32,128]{2,1,0:T(8,128)(2,1)}), bf16[32,32,128]{2,1,0:T(8,128)(2,1)S(1)}, u32[]{:S(2)}, u32[]{:S(2)}) %all-to-all-start) | async-done | bytes 262176 | tf_op jit(solution)/shard_map/all_to_all | solution.py:461
  20.6 0.0 copy-start.1
  20.6 1.2 %shard_map.87 = (f32[256,128]{1,0:T(8,128)S(1)}, bf16[16,72,128]{2,1,0:T(8,128)(2,1)S(1)}) custom-call(bf16[256,1024]{1,0:T(8,128)(2,1)S(1)} %get-tuple-element.23.hidden_ref, bf16[32,32,128]{2,1,0:T(8,128)(2,1)S(1)} %all-to-all-done.w_ref.rest_1_, bf16[1024,1024]{1,0:T(8,128)(2,1)S(1)} %get-tuple-element.25.scaled_t_ref, ...), custom_call_target="tpu_custom_call" | custom-call | tf_op jit(solution)/shard_map/pallas_call | solution.py:488
  21.8 0.0 copy-start.3
  21.8 14.4 %all_to_all.20.in_ref = bf16[16,72,128]{2,1,0:T(8,128)(2,1)S(1)} all-to-all(bf16[16,72,128]{2,1,0:T(8,128)(2,1)S(1)} %get-tuple-element.27), channel_id=1, replica_groups={{0,2,4,6,8,10,12,14,16,18,20,22,24,26,28,30},{1,3,5,7,9,11,13,15,17,19,..., dimensions={0} | all-to-all | bytes 589824 | tf_op jit(solution)/shard_map/all_to_all | solution.py:447
  36.2 1.0 %shard_map.88 = bf16[16,64,128]{2,1,0:T(8,128)(2,1)} custom-call(bf16[16,72,128]{2,1,0:T(8,128)(2,1)S(1)} %all_to_all.20.in_ref), custom_call_target="tpu_custom_call" | custom-call | tf_op jit(solution)/shard_map/pallas_call | solution.py:503
  37.2 3.5 %all-to-all-start.2 = ((bf16[16,64,128]{2,1,0:T(8,128)(2,1)}), bf16[16,64,128]{2,1,0:T(8,128)(2,1)S(1)}, u32[]{:S(2)}, u32[]{:S(2)}) async-start(bf16[16,64,128]{2,1,0:T(8,128)(2,1)} %shard_map.88), calls=%async_computation.2 | async-start | bytes 524288 | tf_op jit(solution)/shard_map/all_to_all | solution.py:447
  40.7 0.0 copy-done.1
  40.7 0.0 copy-start.2
  40.8 0.7 %copy-done.2 = f32[16,256]{1,0:T(8,128)S(1)} copy-done((f32[16,256]{1,0:T(8,128)S(1)}, f32[16,256]{1,0:T(8,128)}, u32[]{:S(2)}) %copy-start.2) | copy-done | bytes 16408
  41.5 4.9 %shard_map.89 = (f32[256,1024]{1,0:T(8,128)}, f32[256,128]{1,0:T(8,128)S(1)}, bf16[1024,1024]{1,0:T(8,128)(2,1)S(1)}) custom-call(f32[256,128]{1,0:T(8,128)S(1)} %get-tuple-element.28.projected_ref, f32[256,256]{1,0:T(8,128)S(1)} %copy-done.1, bf16[256,1024]{1,0:T(8,128)(2,1)} %get-tuple-element.30.x_hbm, bf16[256,1024]{1,0:T(8,128)(2,1)} %get-tuple-element.31.grad_hbm, ...), custom_call_target="tpu_custom_call" | custom-call | tf_op jit(solution)/shard_map/pallas_call | solution.py:494
  46.4 0.0 copy-start.5
  46.4 0.7 copy-done.5
  47.1 3.0 %all-to-all-done.2 = bf16[16,64,128]{2,1,0:T(8,128)(2,1)S(1)} async-done(((bf16[16,64,128]{2,1,0:T(8,128)(2,1)}), bf16[16,64,128]{2,1,0:T(8,128)(2,1)S(1)}, u32[]{:S(2)}, u32[]{:S(2)}) %all-to-all-start.2) | async-done | bytes 262176 | tf_op jit(solution)/shard_map/all_to_all | solution.py:447
  50.1 0.0 copy-start.6
  50.1 0.0 copy-done.3
  50.1 0.0 copy-start
  50.1 2.7 %shard_map.93 = f32[128,1024]{1,0:T(8,128)} custom-call(s32[1]{0:T(128)} %bitcast.place_ref, bf16[1024,128]{1,0:T(8,128)(2,1)S(1)} %bitcast.4, f32[256,128]{1,0:T(8,128)S(1)} %get-tuple-element.28.projected_ref, f32[256,1024]{1,0:T(8,128)} %get-tuple-element.33.d_in_hbm, f32[16,256]{1,0:T(8,128)S(1)} %copy-done.3, f32[16,256]{1,0:T(8,128)S(1)} %get-tuple-element.26.running_t_ref), custom_call_target="tpu_custom_call" | custom-call | tf_op jit(solution)/shard_map/pallas_call | solution.py:521
  52.8 0.0 copy-start.4
  52.8 0.1 collective-permute-start.5
  52.9 0.0 copy-done.6
  52.9 0.8 %shard_map.90.mine_ref = f32[256,128]{1,0:T(8,128)S(1)} custom-call(bf16[1024,128]{1,0:T(8,128)(2,1)S(1)} %bitcast.5, bf16[1024,1024]{1,0:T(8,128)(2,1)S(1)} %get-tuple-element.34.scaled_ref, f32[256,128]{1,0:T(8,128)S(1)} %copy-done.6), custom_call_target="tpu_custom_call" | custom-call | tf_op jit(solution)/shard_map/pallas_call | solution.py:510
  53.7 0.6 collective-permute-start.4
  54.2 1.0 %collective-permute-done.4.other_ref = f32[256,128]{1,0:T(8,128)S(1)} collective-permute-done((f32[256,128]{1,0:T(8,128)S(1)}, f32[256,128]{1,0:T(8,128)S(1)}, u32[]{:S(2)}, u32[]{:S(2)}) %collective-permute-start.4) | collective-permute-done | bytes 131104 | tf_op jit(solution)/shard_map/ppermute | solution.py:452
  55.2 0.0 copy-done
  55.2 0.9 %shard_map.91 = (bf16[256,128]{1,0:T(8,128)(2,1)S(1)}, bf16[16,48,128]{2,1,0:T(8,128)(2,1)}) custom-call(f32[256,128]{1,0:T(8,128)S(1)} %shard_map.90.mine_ref, f32[256,128]{1,0:T(8,128)S(1)} %collective-permute-done.4.other_ref, bf16[512,256]{1,0:T(8,128)(2,1)S(1)} %copy-done), custom_call_target="tpu_custom_call" | custom-call | tf_op jit(solution)/shard_map/pallas_call | solution.py:512
  56.1 3.9 %all-to-all-start.3 = ((bf16[16,48,128]{2,1,0:T(8,128)(2,1)}), bf16[16,48,128]{2,1,0:T(8,128)(2,1)S(1)}, u32[]{:S(2)}, u32[]{:S(2)}) async-start(bf16[16,48,128]{2,1,0:T(8,128)(2,1)} %get-tuple-element.40), calls=%async_computation.3 | async-start | bytes 393216 | tf_op jit(solution)/shard_map/all_to_all | solution.py:447
  60.0 0.0 copy-done.4
  60.0 2.5 %shard_map.92 = (f32[128,1024]{1,0:T(8,128)S(1)}, f32[128,1024]{1,0:T(8,128)}) custom-call(s32[1]{0:T(128)} %bitcast.place_ref, bf16[1024,128]{1,0:T(8,128)(2,1)S(1)} %bitcast.6, f32[256,128]{1,0:T(8,128)S(1)} %get-tuple-element.28.projected_ref, f32[256,1024]{1,0:T(8,128)} %get-tuple-element.33.d_in_hbm, f32[16,256]{1,0:T(8,128)S(1)} %copy-done.4, ...), custom_call_target="tpu_custom_call" | custom-call | tf_op jit(solution)/shard_map/pallas_call | solution.py:526
  62.5 6.7 %all-to-all-done.3.terms_ref = bf16[16,48,128]{2,1,0:T(8,128)(2,1)S(1)} async-done(((bf16[16,48,128]{2,1,0:T(8,128)(2,1)}), bf16[16,48,128]{2,1,0:T(8,128)(2,1)S(1)}, u32[]{:S(2)}, u32[]{:S(2)}) %all-to-all-start.3) | async-done | bytes 196640 | tf_op jit(solution)/shard_map/all_to_all | solution.py:447
  69.2 0.6 shard_map.95
  69.8 0.0 collective-permute-done.5.other_ref
  69.8 1.0 %shard_map.94 = f32[128,2048]{1,0:T(8,128)} custom-call(s32[1]{0:T(128)} %bitcast.place_ref, f32[128,1024]{1,0:T(8,128)S(1)} %get-tuple-element.38.mine_ref, f32[128,1024]{1,0:T(8,128)S(1)} %collective-permute-done.5.other_ref), custom_call_target="tpu_custom_call" | custom-call | tf_op jit(solution)/shard_map/pallas_call | solution.py:530
Async XLA Ops:
  0.6 11.3 %collective-permute-start = (bf16[128,2048]{1,0:T(8,128)(2,1)}, bf16[128,2048]{1,0:T(8,128)(2,1)S(1)}, u32[]{:S(2)}, u32[]{:S(2)}) collective-permute-start(bf16[128,2048]{1,0:T(8,128)(2,1)} %x_hbm.1), channel_id=1, source_target_pairs={{0,1},{1,0},{2,3},{3,2},{4,5},{5,4},{6,7},{7,6},{8,9},{9,8},{10,11... | collective-permute-start | bytes 1572872 | tf_op jit(solution)/shard_map/ppermute | solution.py:452
  1.2 10.7 %collective-permute-start.1 = (bf16[128,2048]{1,0:T(8,128)(2,1)}, bf16[128,2048]{1,0:T(8,128)(2,1)S(1)}, u32[]{:S(2)}, u32[]{:S(2)}) collective-permute-start(bf16[128,2048]{1,0:T(8,128)(2,1)} %grad_hbm.1), channel_id=1, source_target_pairs={{0,1},{1,0},{2,3},{3,2},{4,5},{5,4},{6,7},{7,6},{8,9},{9,8},{10,11... | collective-permute-start | bytes 1572872 | tf_op jit(solution)/shard_map/ppermute | solution.py:452
  2.7 17.8 %all-to-all-start = ((bf16[32,32,128]{2,1,0:T(8,128)(2,1)}), bf16[32,32,128]{2,1,0:T(8,128)(2,1)S(1)}, u32[]{:S(2)}, u32[]{:S(2)}) async-start(bf16[32,32,128]{2,1,0:T(8,128)(2,1)} %get-tuple-element.24), calls=%async_computation | async-start | bytes 524288 | tf_op jit(solution)/shard_map/all_to_all | solution.py:461
  10.0 1.9 %collective-permute-start.3 = (bf16[128,1024]{1,0:T(8,128)(2,1)}, bf16[128,1024]{1,0:T(8,128)(2,1)S(1)}, u32[]{:S(2)}, u32[]{:S(2)}) collective-permute-start(bf16[128,1024]{1,0:T(8,128)(2,1)} %hidden_hbm.1), channel_id=1, source_target_pairs={{0,1},{1,0},{2,3},{3,2},{4,5},{5,4},{6,7},{7,6},{8,9},{9,8},{10,11... | collective-permute-start | bytes 786440 | tf_op jit(solution)/shard_map/ppermute | solution.py:452
  10.3 1.5 %collective-permute-start.2 = (f32[2,32,128]{2,1,0:T(8,128)S(1)}, f32[2,32,128]{2,1,0:T(8,128)S(1)}, u32[]{:S(2)}, u32[]{:S(2)}) collective-permute-start(f32[2,32,128]{2,1,0:T(8,128)S(1)} %get-tuple-element.22.small_ref), channel_id=1, source_target_pairs={{0,1},{1,0},{2,3},{3,2},{4,5},{5,4},{6,7},{7,6},{8,9},{9,8},{10,11... | collective-permute-start | bytes 98312 | tf_op jit(solution)/shard_map/ppermute | solution.py:452
  11.9 0.8 %copy-start.7 = (bf16[128,2048]{1,0:T(8,128)(2,1)}, bf16[128,2048]{1,0:T(8,128)(2,1)S(1)}, u32[]{:S(2)}) copy-start(bf16[128,2048]{1,0:T(8,128)(2,1)S(1)} %collective-permute-done.x_other_hbm) | copy-start | bytes 1572868
  12.7 0.8 %copy-start.8 = (bf16[128,2048]{1,0:T(8,128)(2,1)}, bf16[128,2048]{1,0:T(8,128)(2,1)S(1)}, u32[]{:S(2)}) copy-start(bf16[128,2048]{1,0:T(8,128)(2,1)S(1)} %collective-permute-done.1.grad_other_hbm) | copy-start | bytes 1572868
  20.6 20.1 %copy-start.1 = (f32[256,256]{1,0:T(8,128)S(1)}, f32[256,256]{1,0:T(8,128)}, u32[]{:S(2)}) copy-start(f32[256,256]{1,0:T(8,128)} %get-tuple-element.29.pair_ref) | copy-start | bytes 786436
  21.8 28.2 %copy-start.3 = (f32[16,256]{1,0:T(8,128)S(1)}, f32[16,256]{1,0:T(8,128)}, u32[]{:S(2)}) copy-start(f32[16,256]{1,0:T(8,128)} %get-tuple-element.32.dt_t_ref) | copy-start | bytes 49156
  37.2 12.9 %all-to-all-start.2 = ((bf16[16,64,128]{2,1,0:T(8,128)(2,1)}), bf16[16,64,128]{2,1,0:T(8,128)(2,1)S(1)}, u32[]{:S(2)}, u32[]{:S(2)}) async-start(bf16[16,64,128]{2,1,0:T(8,128)(2,1)} %shard_map.88), calls=%async_computation.2 | async-start | bytes 524288 | tf_op jit(solution)/shard_map/all_to_all | solution.py:447
  40.7 0.7 %copy-start.2 = (f32[16,256]{1,0:T(8,128)S(1)}, f32[16,256]{1,0:T(8,128)}, u32[]{:S(2)}) copy-start(f32[16,256]{1,0:T(8,128)} %get-tuple-element.32.dt_t_ref) | copy-start | bytes 49156
  46.4 0.7 copy-start.5
  50.1 2.8 %copy-start.6 = (f32[256,128]{1,0:T(8,128)S(1)}, f32[256,128]{1,0:T(8,128)}, u32[]{:S(2)}) copy-start(f32[256,128]{1,0:T(8,128)} %copy-done.5) | copy-start | bytes 393220
  50.1 5.1 %copy-start = (bf16[512,256]{1,0:T(8,128)(2,1)S(1)}, bf16[512,256]{1,0:T(8,128)(2,1)}, u32[]{:S(2)}) copy-start(bf16[512,256]{1,0:T(8,128)(2,1)} %get-tuple-element.36.hidden_t_ref) | copy-start | bytes 786436
  52.8 7.2 %copy-start.4 = (f32[16,256]{1,0:T(8,128)S(1)}, f32[16,256]{1,0:T(8,128)}, u32[]{:S(2)}) copy-start(f32[16,256]{1,0:T(8,128)} %get-tuple-element.32.dt_t_ref) | copy-start | bytes 49156
  52.8 17.0 %collective-permute-start.5 = (f32[128,1024]{1,0:T(8,128)}, f32[128,1024]{1,0:T(8,128)S(1)}, u32[]{:S(2)}, u32[]{:S(2)}) collective-permute-start(f32[128,1024]{1,0:T(8,128)} %shard_map.93), channel_id=1, source_target_pairs={{0,1},{1,0},{2,3},{3,2},{4,5},{5,4},{6,7},{7,6},{8,9},{9,8},{10,11... | collective-permute-start | bytes 1572872 | tf_op jit(solution)/shard_map/ppermute | solution.py:452
  53.7 1.5 %collective-permute-start.4 = (f32[256,128]{1,0:T(8,128)S(1)}, f32[256,128]{1,0:T(8,128)S(1)}, u32[]{:S(2)}, u32[]{:S(2)}) collective-permute-start(f32[256,128]{1,0:T(8,128)S(1)} %shard_map.90.mine_ref), channel_id=1, source_target_pairs={{0,1},{1,0},{2,3},{3,2},{4,5},{5,4},{6,7},{7,6},{8,9},{9,8},{10,11... | collective-permute-start | bytes 393224 | tf_op jit(solution)/shard_map/ppermute | solution.py:452
  56.1 13.0 %all-to-all-start.3 = ((bf16[16,48,128]{2,1,0:T(8,128)(2,1)}), bf16[16,48,128]{2,1,0:T(8,128)(2,1)S(1)}, u32[]{:S(2)}, u32[]{:S(2)}) async-start(bf16[16,48,128]{2,1,0:T(8,128)(2,1)} %get-tuple-element.40), calls=%async_computation.3 | async-start | bytes 393216 | tf_op jit(solution)/shard_map/all_to_all | solution.py:447
